TPU v7x, 32 devices: a whole 2x2x4 slice. The times are simulated.
32 devices in a mesh: dp: 16 (over z, x, core), tensor: 2 (over y).
Axes of the slice: x: 2, y: 2, z: 4, core: 2. Of those that a mesh axis runs over, the one named last changes fastest.
Arguments:
- hidden_in: bfloat16 [8192, 768], P(('dp', 'tensor')), may hold values from -6 to 6
- encoder_states: bfloat16 [8192, 768], P(('dp', 'tensor')), may hold values from -6 to 6
- segments: int32 [16, 512], P('dp'), may hold values from 0 to 3, never falling along the last dimension, each value on 1 to 256 neighbouring positions
- buckets: int32 [512], replicated, may hold values from 0 to 31, as said below
- self_qkv: bfloat16 [1, 768, 3, 768], P(None, 'dp', None, 'tensor'), may hold values from -0.109375 to 0.109375
- self_out: bfloat16 [1, 768, 768], P(None, 'tensor', 'dp'), may hold values from -1.25 to 1.25
- cross_q: bfloat16 [1, 768, 768], P(None, 'dp', 'tensor'), may hold values from -0.109375 to 0.109375
- cross_kv: bfloat16 [1, 768, 2, 768], P(None, 'dp', None, 'tensor'), may hold values from -0.109375 to 0.109375
- cross_out: bfloat16 [1, 768, 768], P(None, 'tensor', 'dp'), may hold values from -1.25 to 1.25
- ffn_in: bfloat16 [1, 768, 2, 2048], P(None, 'dp', None, 'tensor'), may hold values from -0.21875 to 0.21875
- ffn_out: bfloat16 [1, 2048, 768], P(None, 'tensor', 'dp'), may hold values from -0.125 to 0.125
- norm_gains: float32 [1, 3, 768], replicated, may hold values from 0.5 to 1.5
- bias_table: float32 [32, 12], replicated, may hold values from -4 to 4
- cotangent: bfloat16 [8192, 768], P(('dp', 'tensor'))
Outputs:
- output: float32 [8192, 768], P(('dp', 'tensor'))
- grad_hidden: float32 [8192, 768], P(('dp', 'tensor'))
- grad_encoder: float32 [8192, 768], P(('dp', 'tensor'))
- grad_self_qkv: float32 [1, 768, 3, 768], P(None, 'dp', None, 'tensor')
- grad_self_out: float32 [1, 768, 768], P(None, 'tensor', 'dp')
- grad_cross_q: float32 [1, 768, 768], P(None, 'dp', 'tensor')
- grad_cross_kv: float32 [1, 768, 2, 768], P(None, 'dp', None, 'tensor')
- grad_cross_out: float32 [1, 768, 768], P(None, 'tensor', 'dp')
- grad_ffn_in: float32 [1, 768, 2, 2048], P(None, 'dp', None, 'tensor')
- grad_ffn_out: float32 [1, 2048, 768], P(None, 'tensor', 'dp')
- grad_gains: float32 [1, 3, 768], replicated
- grad_table: float32 [32, 12], replicated
Inputs may be any that keep to these rules, and one draw needn't show every extreme that they name: `segments`: in each row the document numbers never fall, and no document spans more than 256 positions. buckets[0] is 0, the values never fall and rise by at most 1 from one offset to the next, and the last one is 31.
All inputs are finite; a program needn't handle non-finite values.
Results may differ from a plain program's by a relative error of at most 0.025.
The roundings to bfloat16 on the way count: a program that leaves them out, or rounds other values in their place, can miss the bound.
Values may be sent and summed in bfloat16 or wider, within the bound.
No kernel may reach another device: no remote copies, remote signals or barrier semaphores. Data moves between devices by JAX's collectives and lax.ppermute only.
A program may use at most 128 MiB of HBM per device.

v0:
```python
import jax
import jax.numpy as jnp
from jax import lax
from jax.sharding import PartitionSpec as P

DH = 64


EPSILON = 1e-06
MASKED = -1e30


def normed(features, gain_row):
    return (
        features
        * lax.rsqrt(jnp.mean(features * features, axis=-1, keepdims=True) + EPSILON)
        * gain_row
    )


def gated(gate_part, up_part):
    return jax.nn.gelu(gate_part, approximate=True) * up_part


def spread_rows(features):
    return lax.all_gather(features, "tensor", axis=0, tiled=True)


def reduce_rows(partial_sum):
    return lax.psum_scatter(partial_sum, "tensor", scatter_dimension=0, tiled=True)


def fetch_layer(matrices, layer_index):
    qkv_all, sout_all, cq_all, ckv_all, cout_all, fin_all, fout_all = matrices
    return (
        lax.all_gather(qkv_all[layer_index], "dp", axis=0, tiled=True),
        lax.all_gather(sout_all[layer_index], "dp", axis=1, tiled=True),
        lax.all_gather(cq_all[layer_index], "dp", axis=0, tiled=True),
        lax.all_gather(ckv_all[layer_index], "dp", axis=0, tiled=True),
        lax.all_gather(cout_all[layer_index], "dp", axis=1, tiled=True),
        lax.all_gather(fin_all[layer_index], "dp", axis=0, tiled=True),
        lax.all_gather(fout_all[layer_index], "dp", axis=1, tiled=True),
    )


def head_scores(queries, key_rows, score_bias, allowed):
    scores = (
        jnp.einsum("qhd,khd->hqk", queries, key_rows, preferred_element_type=jnp.float32)
        + score_bias
    )
    if allowed is not None:
        scores = jnp.where(allowed[None], scores, MASKED)
    return scores


def attend(queries, key_rows, value_rows, score_bias, allowed):
    scores = head_scores(queries, key_rows, score_bias, allowed)
    highest = jnp.max(scores, axis=-1, keepdims=True)
    raised = jnp.exp(scores - highest)
    summed = jnp.sum(raised, axis=-1, keepdims=True)
    shares = (raised / summed).astype(jnp.bfloat16)
    mixed_heads = jnp.einsum(
        "hqk,khd->qhd", shares, value_rows, preferred_element_type=jnp.float32
    ).astype(jnp.bfloat16)
    return (mixed_heads, highest + jnp.log(summed))


def attend_back(queries, key_rows, value_rows, score_bias, allowed, log_total, grad_mixed):
    scores = head_scores(queries, key_rows, score_bias, allowed)
    shares = jnp.exp(scores - log_total)
    grad_shares = jnp.einsum(
        "qhd,khd->hqk", grad_mixed, value_rows, preferred_element_type=jnp.float32
    )
    grad_scores = shares * (grad_shares - jnp.sum(shares * grad_shares, axis=-1, keepdims=True))
    rounded = grad_scores.astype(jnp.bfloat16)
    grad_queries = jnp.einsum("hqk,khd->qhd", rounded, key_rows, preferred_element_type=jnp.float32)
    grad_keys = jnp.einsum("hqk,qhd->khd", rounded, queries, preferred_element_type=jnp.float32)
    grad_values = jnp.einsum(
        "hqk,qhd->khd", shares.astype(jnp.bfloat16), grad_mixed, preferred_element_type=jnp.float32
    )
    return (grad_queries, grad_keys, grad_values, grad_scores)


def per_device(
    hidden_in,
    encoder_states,
    segments,
    buckets,
    self_qkv,
    self_out,
    cross_q,
    cross_kv,
    cross_out,
    ffn_in,
    ffn_out,
    norm_gains,
    bias_table,
    cotangent,
):
    matrices = (self_qkv, self_out, cross_q, cross_kv, cross_out, ffn_in, ffn_out)
    layers = self_qkv.shape[0]
    seq_count = segments.shape[0]
    length = segments.shape[1]
    group_rows = seq_count * length
    head_width = self_qkv.shape[-1]
    local_heads = head_width // DH
    bucket_count = bias_table.shape[0]
    first_head = lax.axis_index("tensor") * local_heads
    local_table = lax.dynamic_slice_in_dim(bias_table, first_head, local_heads, 1)
    bucket_ids = jnp.arange(bucket_count, dtype=jnp.int32)
    bucket_first = jnp.sum((buckets[:, None] < bucket_ids[None, :]).astype(jnp.int32), axis=0)
    bucket_span = jnp.sum((buckets[:, None] == bucket_ids[None, :]).astype(jnp.int32), axis=0)
    position = jnp.arange(length, dtype=jnp.int32)
    causal = position[:, None] >= position[None, :]
    block_rows = min(length, 128)
    block_count = length // block_rows

    def onehot_block(block_index):
        rows = block_index * block_rows + jnp.arange(block_rows, dtype=jnp.int32)
        block_offsets = jnp.maximum(rows[:, None] - position[None, :], 0)
        above = block_offsets[:, :, None] - bucket_first[None, None, :]
        return ((above >= 0) & (above < bucket_span[None, None, :])).astype(jnp.float32)

    def bias_block(block_index):
        return jnp.einsum(
            "ijb,bh->hij", onehot_block(block_index), local_table, precision=lax.Precision.HIGHEST
        )

    bias_blocks = lax.map(bias_block, jnp.arange(block_count, dtype=jnp.int32))
    rel_bias = jnp.transpose(bias_blocks, (1, 0, 2, 3)).reshape(local_heads, length, length)

    def self_forward(inputs):
        queries, key_rows, value_rows, segment_row = inputs
        allowed = causal & (segment_row[:, None] == segment_row[None, :])
        return attend(queries, key_rows, value_rows, rel_bias, allowed)

    def cross_forward(inputs):
        queries, key_rows, value_rows = inputs
        return attend(queries, key_rows, value_rows, 0.0, None)

    def self_backward(accumulated, inputs):
        queries, key_rows, value_rows, segment_row, log_total, grad_mixed = inputs
        allowed = causal & (segment_row[:, None] == segment_row[None, :])
        grad_queries, grad_keys, grad_values, grad_scores = attend_back(
            queries, key_rows, value_rows, rel_bias, allowed, log_total, grad_mixed
        )
        return (accumulated + grad_scores, (grad_queries, grad_keys, grad_values))

    def cross_backward(inputs):
        queries, key_rows, value_rows, log_total, grad_mixed = inputs
        grad_queries, grad_keys, grad_values, unused = attend_back(
            queries, key_rows, value_rows, 0.0, None, log_total, grad_mixed
        )
        return (grad_queries, grad_keys, grad_values)

    residual = hidden_in.astype(jnp.float32)
    encoder_rows = spread_rows(encoder_states)
    layer_index = 0
    weights = fetch_layer(matrices, layer_index)
    w_qkv, w_sout, w_cq, w_ckv, w_cout, w_fin, w_fout = weights
    before_self = residual
    normed_self = spread_rows(normed(before_self, norm_gains[layer_index, 0]).astype(jnp.bfloat16))
    projected = jnp.einsum(
        "td,dcf->tcf", normed_self, w_qkv, preferred_element_type=jnp.float32
    ).astype(jnp.bfloat16)
    split_heads = projected.reshape(seq_count, length, 3, local_heads, DH)
    self_mixed, self_log = lax.map(
        self_forward, (split_heads[:, :, 0], split_heads[:, :, 1], split_heads[:, :, 2], segments)
    )
    self_flat = self_mixed.reshape(group_rows, head_width)
    before_cross = before_self + reduce_rows(
        jnp.dot(self_flat, w_sout, preferred_element_type=jnp.float32)
    )
    normed_cross = spread_rows(
        normed(before_cross, norm_gains[layer_index, 1]).astype(jnp.bfloat16)
    )
    cross_queries = jnp.dot(normed_cross, w_cq, preferred_element_type=jnp.float32).astype(
        jnp.bfloat16
    )
    cross_pairs = jnp.einsum(
        "td,dcf->tcf", encoder_rows, w_ckv, preferred_element_type=jnp.float32
    ).astype(jnp.bfloat16)
    pair_heads = cross_pairs.reshape(seq_count, length, 2, local_heads, DH)
    query_heads = cross_queries.reshape(seq_count, length, local_heads, DH)
    cross_mixed, cross_log = lax.map(
        cross_forward, (query_heads, pair_heads[:, :, 0], pair_heads[:, :, 1])
    )
    cross_flat = cross_mixed.reshape(group_rows, head_width)
    before_ffn = before_cross + reduce_rows(
        jnp.dot(cross_flat, w_cout, preferred_element_type=jnp.float32)
    )
    normed_ffn = spread_rows(normed(before_ffn, norm_gains[layer_index, 2]).astype(jnp.bfloat16))
    gate_up = jnp.einsum("td,dcf->tcf", normed_ffn, w_fin, preferred_element_type=jnp.float32)
    activated = gated(gate_up[:, 0], gate_up[:, 1]).astype(jnp.bfloat16)
    residual = before_ffn + reduce_rows(
        jnp.dot(activated, w_fout, preferred_element_type=jnp.float32)
    )
    stored = [
        (
            before_self,
            normed_self,
            split_heads,
            self_flat,
            self_log,
            before_cross,
            normed_cross,
            query_heads,
            pair_heads,
            cross_flat,
            cross_log,
            before_ffn,
            normed_ffn,
            gate_up,
            activated,
        )
    ]
    grad_rows = cotangent.astype(jnp.float32)
    grad_encoder = jnp.zeros((group_rows, encoder_rows.shape[1]), jnp.float32)
    grad_bias = jnp.zeros_like(rel_bias)
    gain_grads = [None] * layers
    weight_grads = [None] * layers
    for layer_index in reversed(range(layers)):
        weights = fetch_layer(matrices, layer_index)
        w_qkv, w_sout, w_cq, w_ckv, w_cout, w_fin, w_fout = weights
        (
            before_self,
            normed_self,
            split_heads,
            self_flat,
            self_log,
            before_cross,
            normed_cross,
            query_heads,
            pair_heads,
            cross_flat,
            cross_log,
            before_ffn,
            normed_ffn,
            gate_up,
            activated,
        ) = stored[layer_index]
        grad_out = spread_rows(grad_rows.astype(jnp.bfloat16))
        grad_act = jnp.einsum("td,fd->tf", grad_out, w_fout, preferred_element_type=jnp.float32)
        unused_value, gate_back = jax.vjp(gated, gate_up[:, 0], gate_up[:, 1])
        grad_gate, grad_up = gate_back(grad_act)
        grad_pair = jnp.stack([grad_gate, grad_up], axis=1).astype(jnp.bfloat16)
        grad_fout = jnp.einsum("tf,td->fd", activated, grad_out, preferred_element_type=jnp.float32)
        grad_fin = jnp.einsum(
            "td,tcf->dcf", normed_ffn, grad_pair, preferred_element_type=jnp.float32
        )
        grad_normed = reduce_rows(
            jnp.einsum("tcf,dcf->td", grad_pair, w_fin, preferred_element_type=jnp.float32)
        )
        unused_value, norm_back = jax.vjp(normed, before_ffn, norm_gains[layer_index, 2])
        grad_prev, gain_ffn = norm_back(grad_normed)
        grad_rows = grad_rows + grad_prev
        grad_out = spread_rows(grad_rows.astype(jnp.bfloat16))
        grad_cmix = jnp.einsum(
            "td,fd->tf", grad_out, w_cout, preferred_element_type=jnp.float32
        ).astype(jnp.bfloat16)
        grad_cout = jnp.einsum(
            "tf,td->fd", cross_flat, grad_out, preferred_element_type=jnp.float32
        )
        grad_cq, grad_ck, grad_cv = lax.map(
            cross_backward,
            (
                query_heads,
                pair_heads[:, :, 0],
                pair_heads[:, :, 1],
                cross_log,
                grad_cmix.reshape(seq_count, length, local_heads, DH),
            ),
        )
        grad_cq_rows = grad_cq.reshape(group_rows, head_width).astype(jnp.bfloat16)
        grad_ckv_rows = (
            jnp.stack([grad_ck, grad_cv], axis=2)
            .reshape(group_rows, 2, head_width)
            .astype(jnp.bfloat16)
        )
        grad_wcq = jnp.einsum(
            "td,tf->df", normed_cross, grad_cq_rows, preferred_element_type=jnp.float32
        )
        grad_wckv = jnp.einsum(
            "td,tcf->dcf", encoder_rows, grad_ckv_rows, preferred_element_type=jnp.float32
        )
        grad_encoder = jnp.einsum(
            "tcf,dcf->td", grad_ckv_rows, w_ckv, preferred_element_type=jnp.float32
        )
        grad_normed = reduce_rows(
            jnp.einsum("tf,df->td", grad_cq_rows, w_cq, preferred_element_type=jnp.float32)
        )
        unused_value, norm_back = jax.vjp(normed, before_cross, norm_gains[layer_index, 1])
        grad_prev, gain_cross = norm_back(grad_normed)
        grad_rows = grad_rows + grad_prev
        grad_out = spread_rows(grad_rows.astype(jnp.bfloat16))
        grad_smix = jnp.einsum(
            "td,fd->tf", grad_out, w_sout, preferred_element_type=jnp.float32
        ).astype(jnp.bfloat16)
        grad_sout = jnp.einsum("tf,td->fd", self_flat, grad_out, preferred_element_type=jnp.float32)
        grad_bias, self_grads = lax.scan(
            self_backward,
            grad_bias,
            (
                split_heads[:, :, 0],
                split_heads[:, :, 1],
                split_heads[:, :, 2],
                segments,
                self_log,
                grad_smix.reshape(seq_count, length, local_heads, DH),
            ),
        )
        grad_proj = (
            jnp.stack([self_grads[0], self_grads[1], self_grads[2]], axis=2)
            .reshape(group_rows, 3, head_width)
            .astype(jnp.bfloat16)
        )
        grad_wqkv = jnp.einsum(
            "td,tcf->dcf", normed_self, grad_proj, preferred_element_type=jnp.float32
        )
        grad_normed = reduce_rows(
            jnp.einsum("tcf,dcf->td", grad_proj, w_qkv, preferred_element_type=jnp.float32)
        )
        unused_value, norm_back = jax.vjp(normed, before_self, norm_gains[layer_index, 0])
        grad_prev, gain_self = norm_back(grad_normed)
        grad_rows = grad_rows + grad_prev
        gain_grads[layer_index] = jnp.stack([gain_self, gain_cross, gain_ffn])
        weight_grads[layer_index] = (
            lax.psum_scatter(grad_wqkv, "dp", scatter_dimension=0, tiled=True),
            lax.psum_scatter(grad_sout, "dp", scatter_dimension=1, tiled=True),
            lax.psum_scatter(grad_wcq, "dp", scatter_dimension=0, tiled=True),
            lax.psum_scatter(grad_wckv, "dp", scatter_dimension=0, tiled=True),
            lax.psum_scatter(grad_cout, "dp", scatter_dimension=1, tiled=True),
            lax.psum_scatter(grad_fin, "dp", scatter_dimension=0, tiled=True),
            lax.psum_scatter(grad_fout, "dp", scatter_dimension=1, tiled=True),
        )
    stacked = tuple((jnp.stack([weight_grads[0][member]]) for member in range(7)))
    grad_blocks = jnp.transpose(
        grad_bias.reshape(local_heads, block_count, block_rows, length), (1, 0, 2, 3)
    )

    def table_block(total, inputs):
        block_index, grad_piece = inputs
        return (
            total
            + jnp.einsum(
                "hij,ijb->bh",
                grad_piece,
                onehot_block(block_index),
                precision=lax.Precision.HIGHEST,
            ),
            None,
        )

    grad_local, unused_rest = lax.scan(
        table_block,
        jnp.zeros((bucket_count, local_heads), jnp.float32),
        (jnp.arange(block_count, dtype=jnp.int32), grad_blocks),
    )
    grad_table = lax.dynamic_update_slice(
        jnp.zeros_like(bias_table), grad_local, (jnp.int32(0), first_head)
    )
    gain_total, table_total = lax.psum((jnp.stack(gain_grads), grad_table), ("dp", "tensor"))
    return (
        residual,
        grad_rows,
        reduce_rows(grad_encoder),
        stacked[0],
        stacked[1],
        stacked[2],
        stacked[3],
        stacked[4],
        stacked[5],
        stacked[6],
        gain_total,
        table_total,
    )


def solution(mesh):
    in_specs = (
        P(("dp", "tensor"), None),
        P(("dp", "tensor"), None),
        P("dp", None),
        P(),
        P(None, "dp", None, "tensor"),
        P(None, "tensor", "dp"),
        P(None, "dp", "tensor"),
        P(None, "dp", None, "tensor"),
        P(None, "tensor", "dp"),
        P(None, "dp", None, "tensor"),
        P(None, "tensor", "dp"),
        P(),
        P(),
        P(("dp", "tensor"), None),
    )
    out_specs = (
        P(("dp", "tensor"), None),
        P(("dp", "tensor"), None),
        P(("dp", "tensor"), None),
        P(None, "dp", None, "tensor"),
        P(None, "tensor", "dp"),
        P(None, "dp", "tensor"),
        P(None, "dp", None, "tensor"),
        P(None, "tensor", "dp"),
        P(None, "dp", None, "tensor"),
        P(None, "tensor", "dp"),
        P(),
        P(),
    )
    return jax.shard_map(
        per_device, mesh=mesh, in_specs=in_specs, out_specs=out_specs, check_vma=False
    )
```

profile of v0, /device:TPU:0, one launch (start us, length us, event | category | flops | bytes accessed | tf_op | source)
XLA Modules:
  0.0 1003.6 jit_solution(2148929955021626212)
XLA Ops:
  14.2 12.8 %all_gather.49 = bf16[512,768]{1,0:T(8,128)(2,1)S(1)} all-gather(bf16[256,768]{1,0:T(8,128)(2,1)S(1)} %fusion.104), channel_id=1, replica_groups=mesh['dp'=16,'tensor'=2] {'tensor'}, dimensions={0}, use_global_device_ids=true | all-gather | bytes 1179648 | tf_op jit(solution)/shard_map/all_gather | solution.py:26
  27.0 23.9 %all-gather.1 = bf16[1,384,768]{1,2,0:T(8,128)(2,1)S(1)} all-gather(bf16[1,384,48]{1,2,0:T(8,128)(2,1)} %param.23), channel_id=3, replica_groups=mesh['dp'=16,'tensor'=2] {'dp'}, dimensions={2}, use_global_device_ids=true | all-gather | bytes 626688 | tf_op jit(solution)/shard_map/all_gather | solution.py:37
  51.0 24.1 %while.6 = (s32[]{:T(128)}, f32[4,6,128,512]{3,1,2,0:T(8,128)}, s32[4]{0:T(128)S(1)}, s32[32]{0:T(128)S(1)}, s32[32]{0:T(128)S(1)}, /*index=5*/f32[32,6]{0,1:T(8,128)S(1)}, s32[]{:T(128)}, s32[1]{0:T(128)}) while((s32[]{:T(128)}, f32[4,6,128,512]{3,1,2,0:T(8,128)}, s32[4]{0:T(128)S(1)}, s32[32]{0:T(128)S(1)}, s32[32]{0:T(128)S(1)}, ...), condition=%wide.region_4.5_spmd.clone, body=%wide.region_3.4_spmd.clone.sunk | while | flops 159514752 | bytes 2623613 | solution.py:129
  52.4 4.6 bitcast_dynamic-update-slice_fusion.2
  58.4 4.7 bitcast_dynamic-update-slice_fusion.2
  64.4 4.6 bitcast_dynamic-update-slice_fusion.2
  70.4 4.7 bitcast_dynamic-update-slice_fusion.2
  75.1 9.7 copy.70
  84.8 2.6 fusion.73
  87.5 4.6 fusion.142
  94.8 2.2 fusion.96
  99.6 19.6 %all_gather.52 = bf16[512,768]{1,0:T(8,128)(2,1)S(1)} all-gather(bf16[256,768]{1,0:T(8,128)(2,1)S(1)} %copy-done.46), channel_id=1, replica_groups=mesh['dp'=16,'tensor'=2] {'tensor'}, dimensions={0}, use_global_device_ids=true | all-gather | bytes 1179648 | tf_op jit(solution)/shard_map/all_gather | solution.py:26
  119.3 19.4 %all-gather.3 = bf16[1,768,384]{2,1,0:T(8,128)(2,1)S(1)} all-gather(bf16[1,48,384]{2,1,0:T(8,128)(2,1)S(1)} %copy-done.58), channel_id=5, replica_groups=mesh['dp'=16,'tensor'=2] {'dp'}, dimensions={1}, use_global_device_ids=true | all-gather | bytes 626688 | tf_op jit(solution)/shard_map/all_gather | solution.py:38
  138.7 20.5 %all-gather.4 = bf16[1,384,768]{1,2,0:T(8,128)(2,1)S(1)} all-gather(bf16[1,384,48]{1,2,0:T(8,128)(2,1)S(1)} %copy-done.59), channel_id=6, replica_groups=mesh['dp'=16,'tensor'=2] {'dp'}, dimensions={2}, use_global_device_ids=true | all-gather | bytes 626688 | tf_op jit(solution)/shard_map/all_gather | solution.py:40
  159.2 5.0 copy.72
  164.2 3.0 convolution_convert_fusion
  169.3 12.8 %all_gather.54 = bf16[512,768]{1,0:T(8,128)(2,1)S(1)} all-gather(bf16[256,768]{1,0:T(8,128)(2,1)S(1)} %multiply_convert_fusion.4), channel_id=1, replica_groups=mesh['dp'=16,'tensor'=2] {'tensor'}, dimensions={0}, use_global_device_ids=true | all-gather | bytes 1179648 | tf_op jit(solution)/shard_map/all_gather | solution.py:26
  191.4 19.8 %all_gather.60 = bf16[512,768]{1,0:T(8,128)(2,1)S(1)} all-gather(bf16[256,768]{1,0:T(8,128)(2,1)S(1)} %copy-done.13), channel_id=1, replica_groups=mesh['dp'=16,'tensor'=2] {'tensor'}, dimensions={0}, use_global_device_ids=true | all-gather | bytes 1179648 | tf_op jit(solution)/shard_map/all_gather | solution.py:26
  211.3 9.8 reduce-scatter.16.cloned.1.call-done
  223.2 11.7 %all_gather.57 = bf16[512,768]{1,0:T(8,128)(2,1)S(1)} all-gather(bf16[256,768]{1,0:T(8,128)(2,1)S(1)} %multiply_convert_fusion.3), channel_id=1, replica_groups=mesh['dp'=16,'tensor'=2] {'tensor'}, dimensions={0}, use_global_device_ids=true | all-gather | bytes 1179648 | tf_op jit(solution)/shard_map/all_gather | solution.py:26
  234.8 31.8 %all-gather.16.cloned.1.call-done = bf16[1,768,2,1024]{3,1,2,0:T(8,128)(2,1)} async-done(((bf16[1,48,2,1024]{3,1,2,0:T(8,128)(2,1)}), bf16[1,768,2,1024]{3,1,2,0:T(8,128)(2,1)}) %all-gather.16.cloned.1.call-update) | async-done | bytes 3145744 | tf_op jit(solution)/shard_map/all_gather | solution.py:41
  266.6 5.7 fusion.48
  272.2 34.4 %all-gather.18.cloned.1.call-done = bf16[1,1024,768]{1,2,0:T(8,128)(2,1)} async-done(((bf16[1,1024,48]{1,2,0:T(8,128)(2,1)}), bf16[1,1024,768]{1,2,0:T(8,128)(2,1)}) %all-gather.18.cloned.1.call-update) | async-done | bytes 1572880 | tf_op jit(solution)/shard_map/all_gather | solution.py:42
  306.7 5.5 fusion.101
  313.6 3.0 fusion.79
  316.7 24.9 %reduce-scatter.20.cloned.1.call-done = f32[256,768]{1,0:T(8,128)} async-done(((f32[512,768]{1,0:T(8,128)}), f32[256,768]{1,0:T(8,128)}) %reduce-scatter.20.cloned.1.call-update) | async-done | bytes 786448 | tf_op jit(solution)/shard_map/reduce_scatter | solution.py:30
  345.0 11.5 %all_gather.61 = bf16[512,768]{1,0:T(8,128)(2,1)S(1)} all-gather(bf16[256,768]{1,0:T(8,128)(2,1)S(1)} %fusion.139), channel_id=1, replica_groups=mesh['dp'=16,'tensor'=2] {'tensor'}, dimensions={0}, use_global_device_ids=true | all-gather | bytes 1179648 | tf_op jit(solution)/shard_map/all_gather | solution.py:26
  357.5 4.3 multiply_reduce_fusion.1
  362.2 2.5 multiply_convert_fusion
  368.1 3.9 fusion.67
  372.1 5.2 fusion.89
  379.2 2.8 convolution_convert_fusion.1
  383.2 2.2 convolution_bitcast_fusion
  385.4 3.1 copy.87
  388.6 6.3 fusion.82
  397.5 25.3 %reduce-scatter.18.cloned.1.call-done = f32[256,768]{1,0:T(8,128)} async-done(((f32[512,768]{1,0:T(8,128)}), f32[256,768]{1,0:T(8,128)}) %reduce-scatter.18.cloned.1.call-update) | async-done | bytes 786448 | tf_op jit(solution)/shard_map/reduce_scatter | solution.py:30
  422.8 3.0 fusion.140
  425.8 11.6 %all_gather.62 = bf16[512,768]{1,0:T(8,128)(2,1)S(1)} all-gather(bf16[256,768]{1,0:T(8,128)(2,1)S(1)} %get-tuple-element.309), channel_id=1, replica_groups=mesh['dp'=16,'tensor'=2] {'tensor'}, dimensions={0}, use_global_device_ids=true | all-gather | bytes 1179648 | tf_op jit(solution)/shard_map/all_gather | solution.py:26
  437.9 4.9 fusion.92
  444.9 5.2 multiply_reduce_fusion
  451.5 2.4 fusion.83
  455.0 3.6 fusion.86
  459.6 4.3 fusion.76
  464.1 2.8 fusion.149
  468.0 2.6 fusion.148
  472.4 3.5 convolution_bitcast_fusion.1
  478.0 4.0 fusion.115
  483.9 41.5 %all-reduce.4.cloned.1.call-done = f32[768,2,384]{2,1,0:T(2,128)} async-done(((f32[768,2,384]{2,1,0:T(2,128)}), f32[768,2,384]{2,1,0:T(2,128)}) %all-reduce.4.cloned.1.call-update) | async-done | bytes 2359312
  527.1 9.9 copy.107
  537.0 32.1 %while.7 = (s32[]{:T(128)}, f32[32,6]{0,1:T(8,128)S(1)}, s32[4]{0:T(128)S(1)}, s32[32]{0:T(128)S(1)}, s32[32]{0:T(128)S(1)}, /*index=5*/f32[4,6,128,512]{3,1,2,0:T(8,128)}, s32[]{:T(128)}, s32[1]{0:T(128)}, s32[]{:T(128)}) while((s32[]{:T(128)}, f32[32,6]{0,1:T(8,128)S(1)}, s32[4]{0:T(128)S(1)}, s32[32]{0:T(128)S(1)}, ...), condition=%wide.region_35.36_spmd.clone, body=%wide.region_34.35_spmd.clone.sunk | while | flops 159515136 | bytes 2624399 | solution.py:354
  538.4 6.7 fusion.187
  546.5 6.7 fusion.187
  554.6 6.6 fusion.187
  562.6 6.6 fusion.187
  569.3 44.1 %reduce-scatter.36.cloned.1.call-done = f32[48,2,1024]{2,0,1:T(8,128)} async-done(((f32[768,2,1024]{2,0,1:T(8,128)}), f32[48,2,1024]{2,0,1:T(8,128)}) %reduce-scatter.36.cloned.1.call-update) | async-done | bytes 393232 | tf_op jit(solution)/shard_map/reduce_scatter | solution.py:333
  615.5 25.3 %reduce-scatter.24.cloned.1.call-done = f32[256,768]{1,0:T(8,128)} async-done(((f32[512,768]{1,0:T(8,128)}), f32[256,768]{1,0:T(8,128)}) %reduce-scatter.24.cloned.1.call-update) | async-done | bytes 786448 | tf_op jit(solution)/shard_map/reduce_scatter | solution.py:30
  642.3 40.0 %all-reduce.1 = (f32[1,3,768]{2,0,1:T(1,128)}, f32[32,12]{0,1:T(8,128)}) all-reduce(f32[1,3,768]{2,0,1:T(1,128)S(1)} %stack.81, f32[32,12]{0,1:T(8,128)S(1)} %dynamic_update_slice.30), channel_id=1, replica_groups=mesh['dp'=16,'tensor'=2] {'dp','tensor'}, use_global_device_ids=true, to_apply=%region_33.34 | all-reduce | flops 2688 | bytes 21504 | tf_op jit(solution)/shard_map/psum | solution.py:362
  682.3 2.3 fusion.108
  684.6 27.7 %reduce-scatter.38.cloned.1.call-done = f32[1024,48]{0,1:T(8,128)} async-done(((f32[1024,768]{0,1:T(8,128)}), f32[1024,48]{0,1:T(8,128)}) %reduce-scatter.38.cloned.1.call-update) | async-done | bytes 196624 | tf_op jit(solution)/shard_map/reduce_scatter | solution.py:334
  712.3 61.1 %reduce-scatter.34.cloned.1.call-done = f32[384,48]{0,1:T(8,128)} async-done(((f32[384,768]{0,1:T(8,128)}), f32[384,48]{0,1:T(8,128)}) %reduce-scatter.34.cloned.1.call-update) | async-done | bytes 73744 | tf_op jit(solution)/shard_map/reduce_scatter | solution.py:332
  773.3 61.3 %reduce-scatter.32.cloned.1.call-done = f32[48,384]{1,0:T(8,128)} async-done(((f32[768,384]{1,0:T(8,128)}), f32[48,384]{1,0:T(8,128)}) %reduce-scatter.32.cloned.1.call-update) | async-done | bytes 73744 | tf_op jit(solution)/shard_map/reduce_scatter | solution.py:330
  834.6 27.9 %reduce-scatter.26.cloned.1.call-done = f32[256,768]{1,0:T(8,128)} async-done(((f32[512,768]{1,0:T(8,128)}), f32[256,768]{1,0:T(8,128)}) %reduce-scatter.26.cloned.1.call-update) | async-done | bytes 786448 | tf_op jit(solution)/shard_map/reduce_scatter | solution.py:30
  862.5 62.3 %reduce-scatter.30.cloned.1.call-done = f32[384,48]{0,1:T(8,128)} async-done(((f32[384,768]{0,1:T(8,128)}), f32[384,48]{0,1:T(8,128)}) %reduce-scatter.30.cloned.1.call-update) | async-done | bytes 73744 | tf_op jit(solution)/shard_map/reduce_scatter | solution.py:329
  924.8 71.5 %reduce-scatter.28.cloned.1.call-done = f32[48,3,384]{2,0,1:T(8,128)} async-done(((f32[768,3,384]{2,0,1:T(8,128)}), f32[48,3,384]{2,0,1:T(8,128)}) %reduce-scatter.28.cloned.1.call-update) | async-done | bytes 221200 | tf_op jit(solution)/shard_map/reduce_scatter | solution.py:328
  (292 shorter events, 63.8 us)
Async XLA Ops:
  7.2 43.8 %copy-start = (f32[32,12]{0,1:T(8,128)S(1)}, f32[32,12]{0,1:T(8,128)}, u32[]{:S(2)}) copy-start(f32[32,12]{0,1:T(8,128)} %param.30) | copy-start | bytes 4612
  7.2 77.6 %all-gather.12.cloned.1.call-start = ((), (), s32[]{:S(2)}) async-start(), calls=%async_computation.26 | async-start | bytes 1880064 | tf_op jit(solution)/shard_map/all_gather | solution.py:36
  7.9 151.3 %all-gather.14.cloned.1.call-start = ((), (), s32[]{:S(2)}) async-start(), calls=%async_computation.27 | async-start | bytes 1253376 | tf_op jit(solution)/shard_map/all_gather | solution.py:39
  8.7 158.5 %reduce-scatter.14.cloned.1.call-start = ((), (), s32[]{:S(2)}) async-start(), calls=%async_computation.13 | async-start | bytes 2359296 | tf_op jit(solution)/shard_map/reduce_scatter | solution.py:30
  27.0 57.8 %copy-start.41 = (bf16[512,768]{1,0:T(8,128)(2,1)}, bf16[512,768]{1,0:T(8,128)(2,1)S(1)}, u32[]{:S(2)}) copy-start(bf16[512,768]{1,0:T(8,128)(2,1)S(1)} %all_gather.49) | copy-start | bytes 2359300
  51.0 46.1 %copy-start.25 = (bf16[1,384,768]{1,2,0:T(8,128)(2,1)}, bf16[1,384,768]{1,2,0:T(8,128)(2,1)S(1)}, u32[]{:S(2)}) copy-start(bf16[1,384,768]{1,2,0:T(8,128)(2,1)S(1)} %all-gather.1) | copy-start | bytes 1769476
  75.1 9.7 copy-start.73
  75.1 9.7 copy-start.75
  87.5 6.2 copy-start.15
  97.0 22.3 %copy-start.58 = (bf16[1,48,384]{2,1,0:T(8,128)(2,1)S(1)}, bf16[1,48,384]{2,1,0:T(8,128)(2,1)}, u32[]{:S(2)}) copy-start(bf16[1,48,384]{2,1,0:T(8,128)(2,1)} %param.24) | copy-start | bytes 110596
  97.0 41.7 %copy-start.59 = (bf16[1,384,48]{1,2,0:T(8,128)(2,1)S(1)}, bf16[1,384,48]{1,2,0:T(8,128)(2,1)}, u32[]{:S(2)}) copy-start(bf16[1,384,48]{1,2,0:T(8,128)(2,1)} %param.26) | copy-start | bytes 110596
  99.6 121.5 %reduce-scatter.16.cloned.1.call-start = ((), (), s32[]{:S(2)}) async-start(), calls=%async_computation.14 | async-start | bytes 2359296 | tf_op jit(solution)/shard_map/reduce_scatter | solution.py:30
  119.3 47.9 %copy-start.22 = (bf16[512,768]{1,0:T(8,128)(2,1)}, bf16[512,768]{1,0:T(8,128)(2,1)S(1)}, u32[]{:S(2)}) copy-start(bf16[512,768]{1,0:T(8,128)(2,1)S(1)} %all_gather.52) | copy-start | bytes 2359300
  138.7 43.4 %copy-start.27 = (bf16[1,768,384]{2,1,0:T(8,128)(2,1)}, bf16[1,768,384]{2,1,0:T(8,128)(2,1)S(1)}, u32[]{:S(2)}) copy-start(bf16[1,768,384]{2,1,0:T(8,128)(2,1)S(1)} %all-gather.3) | copy-start | bytes 1769476
  159.2 29.0 %copy-start.29 = (bf16[1,384,768]{1,2,0:T(8,128)(2,1)}, bf16[1,384,768]{1,2,0:T(8,128)(2,1)S(1)}, u32[]{:S(2)}) copy-start(bf16[1,384,768]{1,2,0:T(8,128)(2,1)S(1)} %all-gather.4) | copy-start | bytes 1769476
  159.2 8.0 copy-start.9
  164.2 4.9 copy-start.57
  167.2 15.4 %copy-start.31 = (bf16[512,2,384]{0,2,1:T(8,128)(2,1)S(1)}, bf16[512,2,384]{0,2,1:T(8,128)(2,1)}, u32[]{:S(2)}) copy-start(bf16[512,2,384]{0,2,1:T(8,128)(2,1)} %convolution_convert_fusion) | copy-start | bytes 2359300
  168.6 52.5 %copy-start.5 = (f32[256,768]{1,0:T(8,128)}, f32[256,768]{1,0:T(8,128)S(1)}, u32[]{:S(2)}) copy-start(f32[256,768]{1,0:T(8,128)S(1)} %get-tuple-element.314) | copy-start | bytes 2359300
  168.6 15.0 %copy-start.63 = (f32[256]{0:T(256)}, f32[256]{0:T(256)S(1)}, u32[]{:S(2)}) copy-start(f32[256]{0:T(256)S(1)} %fusion.131) | copy-start | bytes 3076
  188.2 34.3 %copy-start.38 = (bf16[6,64,512]{2,1,0:T(8,128)(2,1)}, bf16[6,64,512]{2,1,0:T(8,128)(2,1)S(1)}, u32[]{:S(2)}) copy-start(bf16[6,64,512]{2,1,0:T(8,128)(2,1)S(1)} %fusion.95) | copy-start | bytes 1179652
  190.0 76.6 %all-gather.16.cloned.1.call-start = ((), (), s32[]{:S(2)}) async-start(), calls=%async_computation.28 | async-start | bytes 3342336 | tf_op jit(solution)/shard_map/all_gather | solution.py:41
  190.8 115.9 %all-gather.18.cloned.1.call-start = ((), (), s32[]{:S(2)}) async-start(), calls=%async_computation.29 | async-start | bytes 1671168 | tf_op jit(solution)/shard_map/all_gather | solution.py:42
  191.4 150.2 %reduce-scatter.20.cloned.1.call-start = ((), (), s32[]{:S(2)}) async-start(), calls=%async_computation.16 | async-start | bytes 2359296 | tf_op jit(solution)/shard_map/reduce_scatter | solution.py:30
  211.3 95.4 %copy-start.16 = (bf16[512,768]{1,0:T(8,128)(2,1)}, bf16[512,768]{1,0:T(8,128)(2,1)S(1)}, u32[]{:S(2)}) copy-start(bf16[512,768]{1,0:T(8,128)(2,1)S(1)} %all_gather.60) | copy-start | bytes 2359300
  222.5 121.1 %copy-start.7 = (f32[256,768]{1,0:T(8,128)}, f32[256,768]{1,0:T(8,128)S(1)}, u32[]{:S(2)}) copy-start(f32[256,768]{1,0:T(8,128)S(1)} %get-tuple-element.312) | copy-start | bytes 2359300
  234.8 37.4 %copy-start.43 = (bf16[512,768]{1,0:T(8,128)(2,1)}, bf16[512,768]{1,0:T(8,128)(2,1)S(1)}, u32[]{:S(2)}) copy-start(bf16[512,768]{1,0:T(8,128)(2,1)S(1)} %all_gather.57) | copy-start | bytes 2359300
  306.7 6.9 copy-start.77
  316.5 27.0 %copy-start.70 = (f32[256]{0:T(256)S(1)}, f32[256]{0:T(256)}, u32[]{:S(2)}) copy-start(f32[256]{0:T(256)} %copy-done.69) | copy-start | bytes 3076
  316.5 40.0 %copy-start.30 = (bf16[1,384,768]{1,2,0:T(8,128)(2,1)S(1)}, bf16[1,384,768]{1,2,0:T(8,128)(2,1)}, u32[]{:S(2)}) copy-start(bf16[1,384,768]{1,2,0:T(8,128)(2,1)} %copy-done.29) | copy-start | bytes 1769476
  316.6 79.1 %reduce-scatter.22.cloned.1.call-start = ((), (), s32[]{:S(2)}) async-start(), calls=%async_computation.17 | async-start | bytes 2359296 | tf_op jit(solution)/shard_map/reduce_scatter | solution.py:30
  316.7 40.8 %copy-start.47 = (f32[6,512]{1,0:T(8,128)}, f32[6,512]{1,0:T(8,128)S(1)}, u32[]{:S(2)}) copy-start(f32[6,512]{1,0:T(8,128)S(1)} %log_add_fusion.1) | copy-start | bytes 36868
  316.7 40.8 %copy-start.32 = (bf16[512,2,384]{0,2,1:T(8,128)(2,1)S(1)}, bf16[512,2,384]{0,2,1:T(8,128)(2,1)}, u32[]{:S(2)}) copy-start(bf16[512,2,384]{0,2,1:T(8,128)(2,1)} %convolution_convert_fusion) | copy-start | bytes 2359300
  343.6 18.1 %copy-start.71 = (f32[256]{0:T(256)}, f32[256]{0:T(256)S(1)}, u32[]{:S(2)}) copy-start(f32[256]{0:T(256)S(1)} %multiply_multiply_fusion.5) | copy-start | bytes 3076
  357.4 4.3 copy-start.34
  357.4 4.3 slice-start
  357.4 4.8 slice-start.1
  368.1 54.7 %reduce-scatter.18.cloned.1.call-start = ((), (), s32[]{:S(2)}) async-start(), calls=%async_computation.15 | async-start | bytes 2359296 | tf_op jit(solution)/shard_map/reduce_scatter | solution.py:30
  372.0 153.4 %all-reduce.4.cloned.1.call-start = ((), (), s32[]{:S(2)}) async-start(), calls=%async_computation.30 | async-start | bytes 4718592
  383.2 5.3 copy-start.40
  388.6 224.8 %reduce-scatter.36.cloned.1.call-start = ((), (), s32[]{:S(2)}) async-start(), calls=%async_computation.24 | async-start | bytes 6684672 | tf_op jit(solution)/shard_map/reduce_scatter | solution.py:333
  394.9 27.8 %copy-start.8 = (f32[256,768]{1,0:T(8,128)S(1)}, f32[256,768]{1,0:T(8,128)}, u32[]{:S(2)}) copy-start(f32[256,768]{1,0:T(8,128)} %copy-done.7) | copy-start | bytes 2359300
  395.0 27.8 %copy-start.10 = (f32[256,768]{1,0:T(8,128)S(1)}, f32[256,768]{1,0:T(8,128)}, u32[]{:S(2)}) copy-start(f32[256,768]{1,0:T(8,128)} %reduce-scatter.20.cloned.1.call-done) | copy-start | bytes 2359300
  395.0 27.8 %copy-start.14 = (bf16[256,768]{1,0:T(8,128)(2,1)S(1)}, bf16[256,768]{1,0:T(8,128)(2,1)}, u32[]{:S(2)}) copy-start(bf16[256,768]{1,0:T(8,128)(2,1)} %param.31) | copy-start | bytes 1179652
  395.0 27.8 %copy-start.72 = (f32[256]{0:T(256)S(1)}, f32[256]{0:T(256)}, u32[]{:S(2)}) copy-start(f32[256]{0:T(256)} %copy-done.71) | copy-start | bytes 3076
  395.0 245.8 %reduce-scatter.24.cloned.1.call-start = ((), (), s32[]{:S(2)}) async-start(), calls=%async_computation.18 | async-start | bytes 2359296 | tf_op jit(solution)/shard_map/reduce_scatter | solution.py:30
  422.8 14.6 %copy-start.26 = (bf16[1,384,768]{1,2,0:T(8,128)(2,1)S(1)}, bf16[1,384,768]{1,2,0:T(8,128)(2,1)}, u32[]{:S(2)}) copy-start(bf16[1,384,768]{1,2,0:T(8,128)(2,1)} %copy-done.25) | copy-start | bytes 1769476
  437.9 4.9 copy-start.35
  442.8 7.3 slice-start.2
  444.9 5.2 slice-start.3
  459.6 4.4 copy-start.17
  459.6 4.4 copy-start.24
  464.0 248.3 %reduce-scatter.38.cloned.1.call-start = ((), (), s32[]{:S(2)}) async-start(), calls=%async_computation.25 | async-start | bytes 3342336 | tf_op jit(solution)/shard_map/reduce_scatter | solution.py:334
  466.8 306.5 %reduce-scatter.34.cloned.1.call-start = ((), (), s32[]{:S(2)}) async-start(), calls=%async_computation.23 | async-start | bytes 1253376 | tf_op jit(solution)/shard_map/reduce_scatter | solution.py:332
  470.6 364.0 %reduce-scatter.32.cloned.1.call-start = ((), (), s32[]{:S(2)}) async-start(), calls=%async_computation.22 | async-start | bytes 1253376 | tf_op jit(solution)/shard_map/reduce_scatter | solution.py:330
  472.3 390.2 %reduce-scatter.26.cloned.1.call-start = ((), (), s32[]{:S(2)}) async-start(), calls=%async_computation.19 | async-start | bytes 2359296 | tf_op jit(solution)/shard_map/reduce_scatter | solution.py:30
  475.9 448.9 %reduce-scatter.30.cloned.1.call-start = ((), (), s32[]{:S(2)}) async-start(), calls=%async_computation.21 | async-start | bytes 1253376 | tf_op jit(solution)/shard_map/reduce_scatter | solution.py:329
  477.6 518.7 %reduce-scatter.28.cloned.1.call-start = ((), (), s32[]{:S(2)}) async-start(), calls=%async_computation.20 | async-start | bytes 3760128 | tf_op jit(solution)/shard_map/reduce_scatter | solution.py:328
  527.0 9.9 copy-start.74
  527.0 9.9 copy-start.76
  537.0 103.8 %copy-start.61 = (f32[256]{0:T(256)S(1)}, f32[256]{0:T(256)}, u32[]{:S(2)}) copy-start(f32[256]{0:T(256)} %copy-done.60) | copy-start | bytes 3076
  537.0 145.3 %copy-start.68 = (f32[256]{0:T(256)S(1)}, f32[256]{0:T(256)}, u32[]{:S(2)}) copy-start(f32[256]{0:T(256)} %copy-done.67) | copy-start | bytes 3076
  537.0 145.3 %copy-start.23 = (f32[256,768]{1,0:T(8,128)S(1)}, f32[256,768]{1,0:T(8,128)}, u32[]{:S(2)}) copy-start(f32[256,768]{1,0:T(8,128)} %get-tuple-element.310) | copy-start | bytes 2359300
  569.2 427.2 %copy-start.1 = (f32[32,12]{0,1:T(8,128)S(1)}, f32[32,12]{0,1:T(8,128)}, u32[]{:S(2)}) copy-start(f32[32,12]{0,1:T(8,128)} %param.30) | copy-start | bytes 4612
  (39 other events, 76.4 us)
Sparse Core Ops, SparseCore 0:
  10.3 44.2 all-gather.11
  56.9 37.5 all-gather.13
  99.7 30.1 reduce-scatter.13
  190.1 30.9 reduce-scatter.15
  223.8 42.7 all-gather.15
  268.7 37.9 all-gather.17
  316.7 24.8 reduce-scatter.19
  368.2 26.1 reduce-scatter.21
  396.6 26.1 reduce-scatter.17
  426.2 99.2 all-reduce.3
  529.4 83.9 reduce-scatter.35
  615.5 25.2 reduce-scatter.23
  645.2 67.0 reduce-scatter.37
  716.3 56.9 reduce-scatter.33
  777.4 57.1 reduce-scatter.31
  837.3 25.2 reduce-scatter.25
  866.6 58.1 reduce-scatter.29
  929.1 67.1 reduce-scatter.27
where the time goes:
time: 1010 us; the launch traced here: 1000 us
  waiting for transfers between devices  551 us (55%)
  blocking collectives  204 us (20%)
  matrix products  143 us (14%)
  local copies, waits for them, and re-layouts  57.4 us (6%)
  other arithmetic  25.7 us (3%)
  between operations  16.4 us (2%)
    reduce_scatter x7, waiting for transfers between devices, reduce_rows(): lax.psum_scatter(partial_sum, 'tensor', scatter_dimension=0, tiled=True)  113 us
    all_gather x7, blocking collectives, spread_rows(): return lax.all_gather(features, 'tensor', axis=0, tiled=True)  99.8 us
    reduce_scatter x1, waiting for transfers between devices, per_device(): lax.psum_scatter(grad_wqkv, 'dp', scatter_dimension=0, tiled=True)  71.5 us
    reduce_scatter x1, waiting for transfers between devices, per_device(): lax.psum_scatter(grad_sout, 'dp', scatter_dimension=1, tiled=True)  62.3 us
    reduce_scatter x1, waiting for transfers between devices, per_device(): lax.psum_scatter(grad_wcq, 'dp', scatter_dimension=0, tiled=True)  61.3 us
    reduce_scatter x1, waiting for transfers between devices, per_device(): lax.psum_scatter(grad_cout, 'dp', scatter_dimension=1, tiled=True)  61.1 us
    reduce_scatter x1, waiting for transfers between devices, per_device(): lax.psum_scatter(grad_fin, 'dp', scatter_dimension=0, tiled=True)  44.1 us
    unnamed x19, waiting for transfers between devices  43.7 us
  transfers between devices with their start and end apart: 18, of which 14 were waited for; matrix products, arithmetic and copies ran while one was open for 19% of the time, Pallas kernels for 0%

commit v1 on v0

v1 whole, which is shorter than its diff:
```python
import jax
import jax.numpy as jnp
from jax import lax
from jax.sharding import PartitionSpec as P

DH = 64


EPSILON = 1e-06
MASKED = -1e30


def normed(features, gain_row):
    return (
        features
        * lax.rsqrt(jnp.mean(features * features, axis=-1, keepdims=True) + EPSILON)
        * gain_row
    )


def gated(gate_part, up_part):
    return jax.nn.gelu(gate_part, approximate=True) * up_part


def swap_rows(block):
    return lax.ppermute(block, "tensor", [(0, 1), (1, 0)])


def spread_rows(block):
    if lax.axis_size("tensor") != 2:
        return lax.all_gather(block, "tensor", axis=0, tiled=True)
    other = swap_rows(block)
    first = lax.axis_index("tensor") == 0
    return jnp.concatenate([jnp.where(first, block, other), jnp.where(first, other, block)], axis=0)


def reduce_rows(rows, product):
    if lax.axis_size("tensor") != 2:
        return lax.psum_scatter(product(rows), "tensor", scatter_dimension=0, tiled=True)
    half = rows.shape[0] // 2
    place = lax.axis_index("tensor")
    theirs = lax.dynamic_slice_in_dim(rows, (1 - place) * half, half, 0)
    arrived = swap_rows(product(theirs).astype(jnp.bfloat16))
    kept = product(lax.dynamic_slice_in_dim(rows, place * half, half, 0))
    return kept + arrived.astype(jnp.float32)


def sum_everywhere(block):
    for axis in ("tensor", "dp"):
        size = lax.axis_size(axis)
        if size & (size - 1):
            block = lax.psum(block, axis)
            continue
        step = 1
        while step < size:
            block = block + lax.ppermute(block, axis, [(i, i ^ step) for i in range(size)])
            step *= 2
    return block


def times(rows, weight):
    return jnp.dot(rows, weight, preferred_element_type=jnp.float32)


def times_t(rows, weight):
    return lax.dot_general(
        rows, weight, (((1,), (1,)), ((), ())), preferred_element_type=jnp.float32
    )


def outer(left, right):
    return lax.dot_general(
        left, right, (((0,), (0,)), ((), ())), preferred_element_type=jnp.float32
    ).astype(jnp.bfloat16)


def gather_all(pieces):
    return lax.all_gather(jnp.concatenate(pieces, axis=1), "dp", axis=0, tiled=True)


def scatter_all(pieces):
    joined = jnp.concatenate(pieces, axis=1)
    return lax.psum_scatter(joined, "dp", scatter_dimension=0, tiled=True).astype(jnp.float32)


def head_scores(queries, key_rows, score_bias, allowed):
    scores = (
        jnp.einsum("qhd,khd->hqk", queries, key_rows, preferred_element_type=jnp.float32)
        + score_bias
    )
    if allowed is not None:
        scores = jnp.where(allowed[None], scores, MASKED)
    return scores


def attend(queries, key_rows, value_rows, score_bias, allowed):
    scores = head_scores(queries, key_rows, score_bias, allowed)
    highest = jnp.max(scores, axis=-1, keepdims=True)
    raised = jnp.exp(scores - highest)
    summed = jnp.sum(raised, axis=-1, keepdims=True)
    shares = (raised / summed).astype(jnp.bfloat16)
    mixed_heads = jnp.einsum(
        "hqk,khd->qhd", shares, value_rows, preferred_element_type=jnp.float32
    ).astype(jnp.bfloat16)
    return (mixed_heads, highest + jnp.log(summed))


def attend_back(queries, key_rows, value_rows, score_bias, allowed, log_total, grad_mixed):
    scores = head_scores(queries, key_rows, score_bias, allowed)
    shares = jnp.exp(scores - log_total)
    grad_shares = jnp.einsum(
        "qhd,khd->hqk", grad_mixed, value_rows, preferred_element_type=jnp.float32
    )
    grad_scores = shares * (grad_shares - jnp.sum(shares * grad_shares, axis=-1, keepdims=True))
    rounded = grad_scores.astype(jnp.bfloat16)
    grad_queries = jnp.einsum("hqk,khd->qhd", rounded, key_rows, preferred_element_type=jnp.float32)
    grad_keys = jnp.einsum("hqk,qhd->khd", rounded, queries, preferred_element_type=jnp.float32)
    grad_values = jnp.einsum(
        "hqk,qhd->khd", shares.astype(jnp.bfloat16), grad_mixed, preferred_element_type=jnp.float32
    )
    return (grad_queries, grad_keys, grad_values, grad_scores)


def per_device(
    hidden_in,
    encoder_states,
    segments,
    buckets,
    self_qkv,
    self_out,
    cross_q,
    cross_kv,
    cross_out,
    ffn_in,
    ffn_out,
    norm_gains,
    bias_table,
    cotangent,
):
    seq_count = segments.shape[0]
    length = segments.shape[1]
    group_rows = seq_count * length
    head_width = self_qkv.shape[-1]
    local_heads = head_width // DH
    bucket_count = bias_table.shape[0]
    first_head = lax.axis_index("tensor") * local_heads
    local_table = lax.dynamic_slice_in_dim(bias_table, first_head, local_heads, 1)
    bucket_ids = jnp.arange(bucket_count, dtype=jnp.int32)
    bucket_first = jnp.sum((buckets[:, None] < bucket_ids[None, :]).astype(jnp.int32), axis=0)
    bucket_span = jnp.sum((buckets[:, None] == bucket_ids[None, :]).astype(jnp.int32), axis=0)
    position = jnp.arange(length, dtype=jnp.int32)
    causal = position[:, None] >= position[None, :]
    block_rows = min(length, 128)
    block_count = length // block_rows
    last_block = block_count - 1

    rows = last_block * block_rows + jnp.arange(block_rows, dtype=jnp.int32)
    above = jnp.maximum(rows[:, None] - position[None, :], 0)[:, :, None] - bucket_first
    onehot = ((above >= 0) & (above < bucket_span)).astype(jnp.float32)
    last_rows = jnp.einsum("ijb,bh->hij", onehot, local_table, precision=lax.Precision.HIGHEST)
    rel_bias = jnp.concatenate(
        [
            jnp.pad(
                last_rows[:, :, (last_block - block) * block_rows :],
                ((0, 0), (0, 0), (0, (last_block - block) * block_rows)),
            )
            for block in range(block_count)
        ],
        axis=1,
    )

    def self_forward(inputs):
        queries, key_rows, value_rows, segment_row = inputs
        allowed = causal & (segment_row[:, None] == segment_row[None, :])
        return attend(queries, key_rows, value_rows, rel_bias, allowed)

    def cross_forward(inputs):
        queries, key_rows, value_rows = inputs
        return attend(queries, key_rows, value_rows, 0.0, None)

    def self_backward(accumulated, inputs):
        queries, key_rows, value_rows, segment_row, log_total, grad_mixed = inputs
        allowed = causal & (segment_row[:, None] == segment_row[None, :])
        grad_queries, grad_keys, grad_values, grad_scores = attend_back(
            queries, key_rows, value_rows, rel_bias, allowed, log_total, grad_mixed
        )
        return (accumulated + grad_scores, (grad_queries, grad_keys, grad_values))

    def cross_backward(inputs):
        queries, key_rows, value_rows, log_total, grad_mixed = inputs
        grad_queries, grad_keys, grad_values, unused = attend_back(
            queries, key_rows, value_rows, 0.0, None, log_total, grad_mixed
        )
        return (grad_queries, grad_keys, grad_values)

    width = head_width
    hidden = ffn_in.shape[-1]
    own = self_qkv.shape[1]
    early = gather_all([self_qkv[0].reshape(own, 3 * width), self_out[0].T])
    late = gather_all(
        [
            cross_q[0],
            cross_kv[0].reshape(own, 2 * width),
            cross_out[0].T,
            ffn_in[0].reshape(own, 2 * hidden),
            ffn_out[0].T,
        ]
    )
    w_qkv, w_sout = early[:, : 3 * width], early[:, 3 * width :]
    w_cq = late[:, :width]
    w_ckv = late[:, width : 3 * width]
    w_cout = late[:, 3 * width : 4 * width]
    w_fin = late[:, 4 * width : 4 * width + 2 * hidden]
    w_fout = late[:, 4 * width + 2 * hidden :]

    before_self = hidden_in.astype(jnp.float32)
    normed_self = spread_rows(normed(before_self, norm_gains[0, 0]).astype(jnp.bfloat16))
    encoder_rows = spread_rows(encoder_states)
    grad_out = spread_rows(cotangent)
    projected = times(normed_self, w_qkv).astype(jnp.bfloat16)
    split_heads = projected.reshape(seq_count, length, 3, local_heads, DH)
    self_mixed, self_log = lax.map(
        self_forward, (split_heads[:, :, 0], split_heads[:, :, 1], split_heads[:, :, 2], segments)
    )
    self_flat = self_mixed.reshape(group_rows, width)
    before_cross = before_self + reduce_rows(self_flat, lambda part: times_t(part, w_sout))
    normed_cross = spread_rows(normed(before_cross, norm_gains[0, 1]).astype(jnp.bfloat16))
    cross_queries = times(normed_cross, w_cq).astype(jnp.bfloat16)
    cross_pairs = times(encoder_rows, w_ckv).astype(jnp.bfloat16)
    pair_heads = cross_pairs.reshape(seq_count, length, 2, local_heads, DH)
    query_heads = cross_queries.reshape(seq_count, length, local_heads, DH)
    cross_mixed, cross_log = lax.map(
        cross_forward, (query_heads, pair_heads[:, :, 0], pair_heads[:, :, 1])
    )
    cross_flat = cross_mixed.reshape(group_rows, width)
    before_ffn = before_cross + reduce_rows(cross_flat, lambda part: times_t(part, w_cout))
    normed_ffn = spread_rows(normed(before_ffn, norm_gains[0, 2]).astype(jnp.bfloat16))
    gate_up = times(normed_ffn, w_fin)
    gate, up = gate_up[:, :hidden], gate_up[:, hidden:]
    activated = gated(gate, up).astype(jnp.bfloat16)
    residual = before_ffn + reduce_rows(activated, lambda part: times_t(part, w_fout))

    grad_rows = cotangent.astype(jnp.float32)
    grad_act = times(grad_out, w_fout)
    unused_value, gate_back = jax.vjp(gated, gate, up)
    grad_gate, grad_up = gate_back(grad_act)
    grad_pair = jnp.concatenate([grad_gate, grad_up], axis=1).astype(jnp.bfloat16)
    grad_normed = reduce_rows(grad_pair, lambda part: times_t(part, w_fin))
    ffn_sums = scatter_all([outer(normed_ffn, grad_pair), outer(grad_out, activated)])
    unused_value, norm_back = jax.vjp(normed, before_ffn, norm_gains[0, 2])
    grad_prev, gain_ffn = norm_back(grad_normed)
    grad_rows = grad_rows + grad_prev

    grad_out = spread_rows(grad_rows.astype(jnp.bfloat16))
    grad_cmix = times(grad_out, w_cout).astype(jnp.bfloat16)
    grad_wcout = outer(grad_out, cross_flat)
    grad_cq, grad_ck, grad_cv = lax.map(
        cross_backward,
        (
            query_heads,
            pair_heads[:, :, 0],
            pair_heads[:, :, 1],
            cross_log,
            grad_cmix.reshape(seq_count, length, local_heads, DH),
        ),
    )
    grad_cq_rows = grad_cq.reshape(group_rows, width).astype(jnp.bfloat16)
    grad_ckv_rows = jnp.concatenate(
        [
            grad_ck.reshape(group_rows, width).astype(jnp.bfloat16),
            grad_cv.reshape(group_rows, width).astype(jnp.bfloat16),
        ],
        axis=1,
    )
    grad_normed = reduce_rows(grad_cq_rows, lambda part: times_t(part, w_cq))
    grad_encoder = reduce_rows(grad_ckv_rows, lambda part: times_t(part, w_ckv))
    grad_wcq = outer(normed_cross, grad_cq_rows)
    grad_wckv = outer(encoder_rows, grad_ckv_rows)
    unused_value, norm_back = jax.vjp(normed, before_cross, norm_gains[0, 1])
    grad_prev, gain_cross = norm_back(grad_normed)
    grad_rows = grad_rows + grad_prev

    grad_out = spread_rows(grad_rows.astype(jnp.bfloat16))
    grad_smix = times(grad_out, w_sout).astype(jnp.bfloat16)
    grad_wsout = outer(grad_out, self_flat)
    grad_bias, self_grads = lax.scan(
        self_backward,
        jnp.zeros_like(rel_bias),
        (
            split_heads[:, :, 0],
            split_heads[:, :, 1],
            split_heads[:, :, 2],
            segments,
            self_log,
            grad_smix.reshape(seq_count, length, local_heads, DH),
        ),
    )
    grad_proj = jnp.concatenate(
        [part.reshape(group_rows, width).astype(jnp.bfloat16) for part in self_grads], axis=1
    )
    grad_wqkv = outer(normed_self, grad_proj)
    rest_sums = scatter_all([grad_wqkv, grad_wsout, grad_wcq, grad_wckv, grad_wcout])
    grad_normed = reduce_rows(grad_proj, lambda part: times_t(part, w_qkv))
    unused_value, norm_back = jax.vjp(normed, before_self, norm_gains[0, 0])
    grad_prev, gain_self = norm_back(grad_normed)
    grad_rows = grad_rows + grad_prev

    folded = sum(
        jnp.pad(
            grad_bias[
                :, block * block_rows : (block + 1) * block_rows, : (block + 1) * block_rows
            ],
            ((0, 0), (0, 0), ((last_block - block) * block_rows, 0)),
        )
        for block in range(block_count)
    )
    grad_local = jnp.einsum("hij,ijb->hb", folded, onehot, precision=lax.Precision.HIGHEST)
    features = before_self.shape[1]
    grad_table = lax.dynamic_update_slice(
        jnp.zeros((bias_table.shape[1], features), jnp.float32),
        grad_local,
        (first_head, jnp.int32(0)),
    )
    small = jnp.concatenate([jnp.stack([gain_self, gain_cross, gain_ffn]), grad_table], axis=0)
    small = sum_everywhere(small)
    edge = 3 * width
    return (
        residual,
        grad_rows,
        grad_encoder,
        rest_sums[:, :edge].reshape(1, own, 3, width),
        rest_sums[:, edge : edge + width].T[None],
        rest_sums[:, edge + width : edge + 2 * width][None],
        rest_sums[:, edge + 2 * width : edge + 4 * width].reshape(1, own, 2, width),
        rest_sums[:, edge + 4 * width :].T[None],
        ffn_sums[:, : 2 * hidden].reshape(1, own, 2, hidden),
        ffn_sums[:, 2 * hidden :].T[None],
        small[None, :3],
        small[3:, :bucket_count].T,
    )


def solution(mesh):
    in_specs = (
        P(("dp", "tensor"), None),
        P(("dp", "tensor"), None),
        P("dp", None),
        P(),
        P(None, "dp", None, "tensor"),
        P(None, "tensor", "dp"),
        P(None, "dp", "tensor"),
        P(None, "dp", None, "tensor"),
        P(None, "tensor", "dp"),
        P(None, "dp", None, "tensor"),
        P(None, "tensor", "dp"),
        P(),
        P(),
        P(("dp", "tensor"), None),
    )
    out_specs = (
        P(("dp", "tensor"), None),
        P(("dp", "tensor"), None),
        P(("dp", "tensor"), None),
        P(None, "dp", None, "tensor"),
        P(None, "tensor", "dp"),
        P(None, "dp", "tensor"),
        P(None, "dp", None, "tensor"),
        P(None, "tensor", "dp"),
        P(None, "dp", None, "tensor"),
        P(None, "tensor", "dp"),
        P(),
        P(),
    )
    return jax.shard_map(
        per_device, mesh=mesh, in_specs=in_specs, out_specs=out_specs, check_vma=False
    )
```

time: 1010 us -> 368 us (0.36)
  waiting for transfers between devices: 551 us -> 166 us
  blocking collectives: 204 us -> 0 us
  matrix products: 143 us -> 98.6 us
  starting transfers between devices: 0.99 us -> 25.4 us
  local copies, waits for them, and re-layouts: 57.4 us -> 35.2 us
    reduce_scatter x13 -> x2, waiting for transfers between devices: 441 us -> 39.7 us  [scatter_all(): lax.psum_scatter(joined, 'dp', scatter_dimension=0, tiled=True)]
    all_gather x10 -> x0, blocking collectives: 164 us -> none  [the longest x7 99.8 us: spread_rows(): return lax.all_gather(features, 'tensor', axis=0, tiled=True)]
    ppermute x0 -> x19, waiting for transfers between devices: none -> 75.5 us  [the longest x14 71 us: swap_rows(): return lax.ppermute(block, 'tensor', [(0, 1), (1, 0)])]
    unnamed x19 -> x4, waiting for transfers between devices: 43.7 us -> 0.07 us
    psum x1 -> x0, blocking collectives: 40 us -> none  [per_device(): lax.psum((jnp.stack(gain_grads), grad_table), ('dp', 'tensor'))]
    dot_general x29 -> x30, matrix products: 105 us -> 74.7 us  [the longest x7 27.4 us: times(): return jnp.dot(rows, weight, preferred_element_type=jnp.float32)]
    ppermute x0 -> x19, starting transfers between devices: none -> 25.3 us  [the longest x14 18.8 us: swap_rows(): return lax.ppermute(block, 'tensor', [(0, 1), (1, 0)])]
    all_gather x4 -> x2, waiting for transfers between devices: 66.2 us -> 50.2 us  [gather_all(): lax.all_gather(jnp.concatenate(pieces, axis=1), 'dp', axis=0, tiled=True)]
  transfers between devices with their start and end apart: 18 -> 23, of which waited for: 14 -> 17; matrix products, arithmetic and copies ran while one was open for 19% -> 31% of each run, Pallas kernels for 0% -> 0%
where the time goes in v1:
time: 368 us; the launch traced here: 361 us
  waiting for transfers between devices  166 us (45%)
  matrix products  98.6 us (27%)
  local copies, waits for them, and re-layouts  35.2 us (10%)
  starting transfers between devices  25.4 us (7%)
  other arithmetic  21.1 us (6%)
  between operations  15.3 us (4%)
    ppermute x14, waiting for transfers between devices, swap_rows(): return lax.ppermute(block, 'tensor', [(0, 1), (1, 0)])  71 us
    all_gather x2, waiting for transfers between devices, gather_all(): lax.all_gather(jnp.concatenate(pieces, axis=1), 'dp', axis=0, tiled=True)  50.2 us
    reduce_scatter x2, waiting for transfers between devices, scatter_all(): lax.psum_scatter(joined, 'dp', scatter_dimension=0, tiled=True)  39.7 us
    dot_general x7, matrix products, times(): return jnp.dot(rows, weight, preferred_element_type=jnp.float32)  27.4 us
    dot_general x14, matrix products, times_t(): lax.dot_general(rows, weight, (((1,), (1,)), ((), ())), preferred_element...  24.6 us
    ppermute x14, starting transfers between devices, swap_rows(): return lax.ppermute(block, 'tensor', [(0, 1), (1, 0)])  18.8 us
    unnamed x133, local copies, waits for them, and re-layouts  14.1 us
    dot_general x7, matrix products, outer(): lax.dot_general(left, right, (((0,), (0,)), ((), ())), preferred_element_...  11.7 us
  transfers between devices with their start and end apart: 23, of which 17 were waited for; matrix products, arithmetic and copies ran while one was open for 31% of the time, Pallas kernels for 0%

profile of v1, /device:TPU:0, one launch (start us, length us, event | category | flops | bytes accessed | tf_op | source)
XLA Modules:
  0.0 361.1 jit_solution(4046489783672468145)
XLA Ops:
  15.4 3.1 collective-permute-start
  18.7 4.7 %fusion.12 = f32[6,128,512]{2,0,1:T(8,128)} fusion(s32[32]{0:T(128)S(1)} %get-tuple-element.169, s32[32]{0:T(128)S(1)} %get-tuple-element.168, s32[128,512]{1,0:T(8,128)S(1)} %subtract_maximum_fusion, f32[32,12]{0,1:T(8,128)S(1)} %copy-done, s32[]{:T(128)S(6)} %select_n.92), kind=kOutput, calls=%fused_computation.31 | convolution fusion | flops 159383552 | bytes 1840132 | tf_op jit(solution)/shard_map/ijb,bh->hij/dot_general | solution.py:160
  23.4 1.8 copy.72
  29.4 26.4 %all-gather.3.cloned.1.call-done = bf16[768,1536]{1,0:T(8,128)(2,1)} async-done(((bf16[48,1536]{1,0:T(8,128)(2,1)}), bf16[768,1536]{1,0:T(8,128)(2,1)}) %all-gather.3.cloned.1.call-update) | async-done | bytes 2359312 | tf_op jit(solution)/shard_map/all_gather | solution.py:78
  55.7 3.7 %convolution_convert_fusion.2 = bf16[512,1152]{1,0:T(8,128)(2,1)} fusion(bf16[768,1536]{1,0:T(8,128)(2,1)} %all-gather.3.cloned.1.call-done, bf16[256,768]{1,0:T(8,128)(2,1)S(1)} %get-tuple-element.190, bf16[256,768]{1,0:T(8,128)(2,1)S(1)} %get-tuple-element.189), kind=kOutput, calls=%fused_computation.43 | convolution fusion | flops 908132352 | bytes 3735552 | tf_op jit(solution)/shard_map/dot_general | solution.py:62
  59.4 1.6 copy.71
  61.0 3.7 %fusion.185 = (f32[6,512]{1,0:T(8,128)S(1)}, f32[6,512,512]{1,2,0:T(8,128)S(1)}) fusion(f32[6,128,512]{1,2,0:T(8,128)S(1)} %copy.72, f32[6,128,384]{1,2,0:T(8,128)} %slice.146, f32[6,128,256]{1,2,0:T(8,128)} %slice.145, f32[6,128,128]{1,2,0:T(8,128)} %slice.144, bf16[1,512,3,6,64]{1,4,3,2,0:T(8,128)(2,1)S(1)} %bitcast.124, pred[512,512]{0,1:T(8,128)(4,1)} %fusion.81), kind=kOutput, calls=%fused_computation.277 | convolution fusion | flops 226489344 | bytes 11284480 | tf_op jit(solution)/shard_map/while/body/eval_jaxpr/qhd,khd->hqk/dot_general | solution.py:88
  65.6 1.8 copy-done.3
  68.6 1.6 convolution_convert_fusion.18
  70.3 1.5 collective-permute-start.1
  72.3 10.0 %collective-permute-done.1 = bf16[256,768]{1,0:T(8,128)(2,1)S(1)} collective-permute-done((bf16[256,768]{1,0:T(8,128)(2,1)S(1)}, bf16[256,768]{1,0:T(8,128)(2,1)S(1)}, u32[]{:S(2)}, u32[]{:S(2)}) %collective-permute-start.1) | collective-permute-done | bytes 393248 | tf_op jit(solution)/shard_map/ppermute | solution.py:26
  82.3 1.7 multiply_reduce_fusion.7
  84.2 1.5 collective-permute-start.3
  85.7 5.0 %collective-permute-done.2 = bf16[256,768]{1,0:T(8,128)(2,1)S(1)} collective-permute-done((bf16[256,768]{1,0:T(8,128)(2,1)S(1)}, bf16[256,768]{1,0:T(8,128)(2,1)S(1)}, u32[]{:S(2)}, u32[]{:S(2)}) %collective-permute-start.2) | collective-permute-done | bytes 393248 | tf_op jit(solution)/shard_map/ppermute | solution.py:26
  90.8 7.6 %collective-permute-done.3 = bf16[256,768]{1,0:T(8,128)(2,1)S(1)} collective-permute-done((bf16[256,768]{1,0:T(8,128)(2,1)S(1)}, bf16[256,768]{1,0:T(8,128)(2,1)S(1)}, u32[]{:S(2)}, u32[]{:S(2)}) %collective-permute-start.3) | collective-permute-done | bytes 393248 | tf_op jit(solution)/shard_map/ppermute | solution.py:26
  99.5 23.8 %all-gather.5.cloned.1.call-done = bf16[768,4608]{1,0:T(8,128)(2,1)} async-done(((bf16[48,4608]{1,0:T(8,128)(2,1)}), bf16[768,4608]{1,0:T(8,128)(2,1)}) %all-gather.5.cloned.1.call-update) | async-done | bytes 7077904 | tf_op jit(solution)/shard_map/all_gather | solution.py:78
  123.4 2.0 convolution_convert_fusion.5
  125.7 1.8 convolution_convert_fusion.15
  129.5 2.3 copy-done.2
  134.6 1.6 collective-permute-start.4
  136.7 10.0 %collective-permute-done.4 = bf16[256,768]{1,0:T(8,128)(2,1)S(1)} collective-permute-done((bf16[256,768]{1,0:T(8,128)(2,1)S(1)}, bf16[256,768]{1,0:T(8,128)(2,1)S(1)}, u32[]{:S(2)}, u32[]{:S(2)}) %collective-permute-start.4) | collective-permute-done | bytes 393248 | tf_op jit(solution)/shard_map/ppermute | solution.py:26
  147.4 1.5 collective-permute-start.5
  148.9 6.2 %collective-permute-done.7 = bf16[256,768]{1,0:T(8,128)(2,1)S(1)} collective-permute-done((bf16[256,768]{1,0:T(8,128)(2,1)S(1)}, bf16[256,768]{1,0:T(8,128)(2,1)S(1)}, u32[]{:S(2)}, u32[]{:S(2)}) %collective-permute-start.7) | collective-permute-done | bytes 393248 | tf_op jit(solution)/shard_map/ppermute | solution.py:26
  155.2 7.6 %collective-permute-done.5 = bf16[256,768]{1,0:T(8,128)(2,1)S(1)} collective-permute-done((bf16[256,768]{1,0:T(8,128)(2,1)S(1)}, bf16[256,768]{1,0:T(8,128)(2,1)S(1)}, u32[]{:S(2)}, u32[]{:S(2)}) %collective-permute-start.5) | collective-permute-done | bytes 393248 | tf_op jit(solution)/shard_map/ppermute | solution.py:26
  163.1 1.8 fusion.27
  164.9 14.2 %multiply_convert_fusion.1 = (bf16[512,1024]{1,0:T(8,128)(2,1)S(1)}, bf16[512,1024]{1,0:T(8,128)(2,1)S(1)}, bf16[512,1024]{1,0:T(8,128)(2,1)S(1)}) fusion(f32[512,2048]{1,0:T(8,128)S(1)} %fusion.27, bf16[768,4608]{1,0:T(8,128)(2,1)S(1)} %bitcast.130, bf16[256,768]{1,0:T(8,128)(2,1)S(1)} %get-tuple-element.182, bf16[256,768]{1,0:T(8,128)(2,1)S(1)} %get-tuple-element.181), kind=kOutput, calls=%fused_computation.62 | convolution fusion | flops 820510720 | bytes 9699328 | tf_op jit(solution)/shard_map/dot_general | solution.py:62
  180.2 1.5 collective-permute-start.8
  181.7 1.8 convolution_convert_fusion
  184.6 6.1 %collective-permute-done.8 = bf16[256,768]{1,0:T(8,128)(2,1)S(1)} collective-permute-done((bf16[256,768]{1,0:T(8,128)(2,1)S(1)}, bf16[256,768]{1,0:T(8,128)(2,1)S(1)}, u32[]{:S(2)}, u32[]{:S(2)}) %collective-permute-start.8) | collective-permute-done | bytes 393248 | tf_op jit(solution)/shard_map/ppermute | solution.py:26
  194.5 2.5 pad_maximum_fusion
  197.1 5.7 %collective-permute-done.9 = bf16[256,768]{1,0:T(8,128)(2,1)S(1)} collective-permute-done((bf16[256,768]{1,0:T(8,128)(2,1)}, bf16[256,768]{1,0:T(8,128)(2,1)S(1)}, u32[]{:S(2)}, u32[]{:S(2)}) %collective-permute-start.9) | collective-permute-done | bytes 393248 | tf_op jit(solution)/shard_map/ppermute | solution.py:26
  203.9 1.9 convolution_convert_fusion.13
  205.8 4.6 %multiply_reduce_fusion.1 = (f32[6,512]{1,0:T(8,128)S(1)}, f32[6,512,512]{1,2,0:T(8,128)S(1)}) fusion(f32[6,512,512]{1,2,0:T(8,128)} %copy-done.2, f32[6,512]{1,0:T(8,128)S(1)} %log_add_fusion.1, bf16[512,6,64]{0,2,1:T(8,128)(2,1)S(1)} %bitcast.131, bf16[1,512,2,6,64]{1,4,3,2,0:T(8,128)(2,1)S(1)} %bitcast.122), kind=kOutput, calls=%fused_computation.17 | convolution fusion | flops 206042112 | bytes 13398016 | tf_op jit(solution)/shard_map/while/body/eval_jaxpr/qhd,khd->hqk/dot_general | solution.py:111
  211.2 1.8 multiply_convert_fusion
  213.6 1.6 convolution_convert_fusion.16
  215.2 1.5 collective-permute-start.10
  216.8 1.8 convolution_convert_fusion.10
  218.6 5.4 %collective-permute-done.10 = bf16[256,768]{1,0:T(8,128)(2,1)S(1)} collective-permute-done((bf16[256,768]{1,0:T(8,128)(2,1)S(1)}, bf16[256,768]{1,0:T(8,128)(2,1)S(1)}, u32[]{:S(2)}, u32[]{:S(2)}) %collective-permute-start.10) | collective-permute-done | bytes 393248 | tf_op jit(solution)/shard_map/ppermute | solution.py:26
  224.0 1.8 multiply_reduce_fusion.3
  228.3 1.9 fusion.61
  230.2 4.5 %collective-permute-done.11 = bf16[256,768]{1,0:T(8,128)(2,1)S(1)} collective-permute-done((bf16[256,768]{1,0:T(8,128)(2,1)S(1)}, bf16[256,768]{1,0:T(8,128)(2,1)S(1)}, u32[]{:S(2)}, u32[]{:S(2)}) %collective-permute-start.11) | collective-permute-done | bytes 393248 | tf_op jit(solution)/shard_map/ppermute | solution.py:26
  234.8 1.9 convolution_convert_fusion.11
  236.8 2.5 multiply_reduce_fusion
  239.2 1.7 subtract_multiply_fusion
  240.9 2.4 fusion.55
  243.6 1.7 fusion.52
  246.7 2.5 fusion.14
  252.3 1.9 fusion.40
  254.2 1.5 fusion.46
  257.0 2.8 convolution_convert_fusion.14
  263.4 1.5 slice.166
  267.6 1.7 slice_add_fusion
  269.3 2.0 copy.89
  271.3 6.4 %fusion.74 = f32[6,32]{1,0:T(8,128)S(1)} fusion(f32[6,128,512]{2,0,1:T(8,128)} %copy.89, s32[32]{0:T(128)S(1)} %get-tuple-element.169, s32[32]{0:T(128)S(1)} %get-tuple-element.168, s32[128,512]{1,0:T(8,128)S(1)} %copy-done.52), kind=kOutput, calls=%fused_computation.117 | convolution fusion | flops 159383552 | bytes 1836032 | tf_op jit(solution)/shard_map/hij,ijb->hb/dot_general | solution.py:317
  278.2 2.6 fusion.89
  280.9 1.6 collective-permute-start.14
  282.5 1.9 convolution_convert_fusion.9
  285.7 3.1 add_add_fusion.3
  289.2 3.0 collective-permute-done.13
  292.2 2.7 convert_add_fusion.1
  294.9 1.6 collective-permute-start.17
  296.6 2.5 collective-permute-done.17
  299.1 2.7 collective-permute-start.18
  309.4 39.7 %reduce-scatter.3.cloned.1.call-done = bf16[48,3072]{1,0:T(8,128)(2,1)} async-done(((bf16[768,3072]{1,0:T(8,128)(2,1)}), bf16[48,3072]{1,0:T(8,128)(2,1)}) %reduce-scatter.3.cloned.1.call-update) | async-done | bytes 294928 | tf_op jit(solution)/shard_map/reduce_scatter | solution.py:83
  (234 shorter events, 60.8 us)
Async XLA Ops:
  7.2 11.5 %copy-start = (f32[32,12]{0,1:T(8,128)S(1)}, f32[32,12]{0,1:T(8,128)}, u32[]{:S(2)}) copy-start(f32[32,12]{0,1:T(8,128)} %param.26) | copy-start | bytes 4612
  7.2 7.8 %copy-start.53 = (f32[1,3,768]{2,0,1:T(1,128)S(1)}, f32[1,3,768]{2,0,1:T(1,128)}, u32[]{:S(2)}) copy-start(f32[1,3,768]{2,0,1:T(1,128)} %param.25) | copy-start | bytes 27652
  7.2 7.8 %copy-start.7 = (bf16[256,768]{1,0:T(8,128)(2,1)S(1)}, bf16[256,768]{1,0:T(8,128)(2,1)}, u32[]{:S(2)}) copy-start(bf16[256,768]{1,0:T(8,128)(2,1)} %param.14) | copy-start | bytes 1179652
  7.2 11.3 %copy-start.55 = (s32[512]{0:T(512)S(1)}, s32[512]{0:T(512)}, u32[]{:S(2)}) copy-start(s32[512]{0:T(512)} %param.17) | copy-start | bytes 6148
  7.2 48.5 %all-gather.3.cloned.1.call-start = ((), (), s32[]{:S(2)}) async-start(), calls=%async_computation.2 | async-start | bytes 2506752 | tf_op jit(solution)/shard_map/all_gather | solution.py:78
  9.8 113.6 %all-gather.5.cloned.1.call-start = ((), (), s32[]{:S(2)}) async-start(), calls=%async_computation.3 | async-start | bytes 7520256 | tf_op jit(solution)/shard_map/all_gather | solution.py:78
  15.0 290.7 %reduce-scatter.5.cloned.1.call-start = ((), (), s32[]{:S(2)}) async-start(), calls=%async_computation.5 | async-start | bytes 5013504 | tf_op jit(solution)/shard_map/reduce_scatter | solution.py:83
  15.4 13.7 %collective-permute-start = (bf16[256,768]{1,0:T(8,128)(2,1)S(1)}, bf16[256,768]{1,0:T(8,128)(2,1)S(1)}, u32[]{:S(2)}, u32[]{:S(2)}) collective-permute-start(bf16[256,768]{1,0:T(8,128)(2,1)S(1)} %fusion.88), channel_id=1, source_target_pairs={{0,1},{1,0},{2,3},{3,2},{4,5},{5,4},{6,7},{7,6},{8,9},{9,8},{10,11... | collective-permute-start | bytes 1179656 | tf_op jit(solution)/shard_map/ppermute | solution.py:26
  18.7 4.7 %copy-start.51 = (s32[128,512]{1,0:T(8,128)}, s32[128,512]{1,0:T(8,128)S(1)}, u32[]{:S(2)}) copy-start(s32[128,512]{1,0:T(8,128)S(1)} %subtract_maximum_fusion) | copy-start | bytes 786436
  25.3 2.9 copy-start.54
  29.4 26.4 %copy-start.24 = (bf16[256,768]{1,0:T(8,128)(2,1)}, bf16[256,768]{1,0:T(8,128)(2,1)S(1)}, u32[]{:S(2)}) copy-start(bf16[256,768]{1,0:T(8,128)(2,1)S(1)} %get-tuple-element.189) | copy-start | bytes 1179652
  29.4 26.4 %copy-start.26 = (bf16[256,768]{1,0:T(8,128)(2,1)}, bf16[256,768]{1,0:T(8,128)(2,1)S(1)}, u32[]{:S(2)}) copy-start(bf16[256,768]{1,0:T(8,128)(2,1)S(1)} %get-tuple-element.190) | copy-start | bytes 1179652
  61.0 4.6 %copy-start.8 = (bf16[512,1152]{0,1:T(8,128)(2,1)}, bf16[512,1152]{0,1:T(8,128)(2,1)S(1)}, u32[]{:S(2)}) copy-start(bf16[512,1152]{0,1:T(8,128)(2,1)S(1)} %copy.71) | copy-start | bytes 3538948
  64.7 2.7 copy-start.3
  67.4 4.4 %copy-start.23 = (bf16[256,768]{1,0:T(8,128)(2,1)S(1)}, bf16[256,768]{1,0:T(8,128)(2,1)}, u32[]{:S(2)}) copy-start(bf16[256,768]{1,0:T(8,128)(2,1)} %param.15) | copy-start | bytes 1179652
  70.3 12.1 %collective-permute-start.1 = (bf16[256,768]{1,0:T(8,128)(2,1)S(1)}, bf16[256,768]{1,0:T(8,128)(2,1)S(1)}, u32[]{:S(2)}, u32[]{:S(2)}) collective-permute-start(bf16[256,768]{1,0:T(8,128)(2,1)S(1)} %convolution_convert_fusion.18), channel_id=1, source_target_pairs={{0,1},{1,0},{2,3},{3,2},{4,5},{5,4},{6,7},{7,6},{8,9},{9,8},{10,11... | collective-permute-start | bytes 1179656 | tf_op jit(solution)/shard_map/ppermute | solution.py:26
  71.8 18.9 %collective-permute-start.2 = (bf16[256,768]{1,0:T(8,128)(2,1)S(1)}, bf16[256,768]{1,0:T(8,128)(2,1)S(1)}, u32[]{:S(2)}, u32[]{:S(2)}) collective-permute-start(bf16[256,768]{1,0:T(8,128)(2,1)S(1)} %copy-done.23), channel_id=1, source_target_pairs={{0,1},{1,0},{2,3},{3,2},{4,5},{5,4},{6,7},{7,6},{8,9},{9,8},{10,11... | collective-permute-start | bytes 1179656 | tf_op jit(solution)/shard_map/ppermute | solution.py:26
  84.2 14.3 %collective-permute-start.3 = (bf16[256,768]{1,0:T(8,128)(2,1)S(1)}, bf16[256,768]{1,0:T(8,128)(2,1)S(1)}, u32[]{:S(2)}, u32[]{:S(2)}) collective-permute-start(bf16[256,768]{1,0:T(8,128)(2,1)S(1)} %multiply_convert_fusion.4), channel_id=1, source_target_pairs={{0,1},{1,0},{2,3},{3,2},{4,5},{5,4},{6,7},{7,6},{8,9},{9,8},{10,11... | collective-permute-start | bytes 1179656 | tf_op jit(solution)/shard_map/ppermute | solution.py:26
  90.8 32.6 %copy-start.30 = (bf16[256,768]{1,0:T(8,128)(2,1)}, bf16[256,768]{1,0:T(8,128)(2,1)S(1)}, u32[]{:S(2)}) copy-start(bf16[256,768]{1,0:T(8,128)(2,1)S(1)} %get-tuple-element.185) | copy-start | bytes 1179652
  90.8 34.6 %copy-start.32 = (bf16[256,768]{1,0:T(8,128)(2,1)}, bf16[256,768]{1,0:T(8,128)(2,1)S(1)}, u32[]{:S(2)}) copy-start(bf16[256,768]{1,0:T(8,128)(2,1)S(1)} %get-tuple-element.186) | copy-start | bytes 1179652
  128.6 3.2 copy-start.2
  128.6 4.5 %slice-start.4 = ((s8[7077888]{0:T(1024)(128)(4,1)}), s8[4194304]{0:T(1024)(128)(4,1)S(1)}, s32[]{:S(2)}) async-start(s8[7077888]{0:T(1024)(128)(4,1)} %bitcast.129), calls=%async_computation.10 | async-start | bytes 8388608
  131.8 4.4 %copy-start.12 = (bf16[256,768]{1,0:T(8,128)(2,1)S(1)}, bf16[256,768]{1,0:T(8,128)(2,1)}, u32[]{:S(2)}) copy-start(bf16[256,768]{1,0:T(8,128)(2,1)} %param.27) | copy-start | bytes 1179652
  133.0 14.3 %copy-start.34 = (bf16[6,64,512]{2,1,0:T(8,128)(2,1)}, bf16[6,64,512]{2,1,0:T(8,128)(2,1)S(1)}, u32[]{:S(2)}) copy-start(bf16[6,64,512]{2,1,0:T(8,128)(2,1)S(1)} %fusion.67) | copy-start | bytes 1179652
  134.6 12.1 %collective-permute-start.4 = (bf16[256,768]{1,0:T(8,128)(2,1)S(1)}, bf16[256,768]{1,0:T(8,128)(2,1)S(1)}, u32[]{:S(2)}, u32[]{:S(2)}) collective-permute-start(bf16[256,768]{1,0:T(8,128)(2,1)S(1)} %convolution_convert_fusion.17), channel_id=1, source_target_pairs={{0,1},{1,0},{2,3},{3,2},{4,5},{5,4},{6,7},{7,6},{8,9},{9,8},{10,11... | collective-permute-start | bytes 1179656 | tf_op jit(solution)/shard_map/ppermute | solution.py:26
  136.2 18.9 %collective-permute-start.7 = (bf16[256,768]{1,0:T(8,128)(2,1)S(1)}, bf16[256,768]{1,0:T(8,128)(2,1)S(1)}, u32[]{:S(2)}, u32[]{:S(2)}) collective-permute-start(bf16[256,768]{1,0:T(8,128)(2,1)S(1)} %copy-done.12), channel_id=1, source_target_pairs={{0,1},{1,0},{2,3},{3,2},{4,5},{5,4},{6,7},{7,6},{8,9},{9,8},{10,11... | collective-permute-start | bytes 1179656 | tf_op jit(solution)/shard_map/ppermute | solution.py:26
  147.2 44.7 %copy-start.5 = (f32[256,768]{1,0:T(8,128)}, f32[256,768]{1,0:T(8,128)S(1)}, u32[]{:S(2)}) copy-start(f32[256,768]{1,0:T(8,128)S(1)} %get-tuple-element.201) | copy-start | bytes 2359300
  147.4 15.4 %collective-permute-start.5 = (bf16[256,768]{1,0:T(8,128)(2,1)S(1)}, bf16[256,768]{1,0:T(8,128)(2,1)S(1)}, u32[]{:S(2)}, u32[]{:S(2)}) collective-permute-start(bf16[256,768]{1,0:T(8,128)(2,1)S(1)} %multiply_convert_fusion.3), channel_id=1, source_target_pairs={{0,1},{1,0},{2,3},{3,2},{4,5},{5,4},{6,7},{7,6},{8,9},{9,8},{10,11... | collective-permute-start | bytes 1179656 | tf_op jit(solution)/shard_map/ppermute | solution.py:26
  179.1 4.5 %copy-start.48 = (bf16[512,1024]{1,0:T(8,128)(2,1)}, bf16[512,1024]{1,0:T(8,128)(2,1)S(1)}, u32[]{:S(2)}) copy-start(bf16[512,1024]{1,0:T(8,128)(2,1)S(1)} %get-tuple-element.176) | copy-start | bytes 3145732
  180.2 10.5 %collective-permute-start.8 = (bf16[256,768]{1,0:T(8,128)(2,1)S(1)}, bf16[256,768]{1,0:T(8,128)(2,1)S(1)}, u32[]{:S(2)}, u32[]{:S(2)}) collective-permute-start(bf16[256,768]{1,0:T(8,128)(2,1)S(1)} %fusion.58), channel_id=1, source_target_pairs={{0,1},{1,0},{2,3},{3,2},{4,5},{5,4},{6,7},{7,6},{8,9},{9,8},{10,11... | collective-permute-start | bytes 1179656 | tf_op jit(solution)/shard_map/ppermute | solution.py:26
  193.0 9.8 %collective-permute-start.9 = (bf16[256,768]{1,0:T(8,128)(2,1)}, bf16[256,768]{1,0:T(8,128)(2,1)S(1)}, u32[]{:S(2)}, u32[]{:S(2)}) collective-permute-start(bf16[256,768]{1,0:T(8,128)(2,1)} %get-tuple-element.172), channel_id=1, source_target_pairs={{0,1},{1,0},{2,3},{3,2},{4,5},{5,4},{6,7},{7,6},{8,9},{9,8},{10,11... | collective-permute-start | bytes 1179656 | tf_op jit(solution)/shard_map/ppermute | solution.py:26
  197.0 152.1 %reduce-scatter.3.cloned.1.call-start = ((), (), s32[]{:S(2)}) async-start(), calls=%async_computation.4 | async-start | bytes 5013504 | tf_op jit(solution)/shard_map/reduce_scatter | solution.py:83
  205.8 4.6 %slice-start = ((s8[6291456]{0:T(1024)(128)(4,1)}), s8[4194304]{0:T(1024)(128)(4,1)S(1)}, s32[]{:S(2)}) async-start(s8[6291456]{0:T(1024)(128)(4,1)} %bitcast.116), calls=%async_computation.6 | async-start | bytes 8388608
  205.8 5.4 %slice-start.1 = ((s8[6291456]{0:T(1024)(128)(4,1)}), s8[2097152]{0:T(1024)(128)(4,1)S(1)}, s32[]{:S(2)}) async-start(s8[6291456]{0:T(1024)(128)(4,1)} %bitcast.116), calls=%async_computation.7 | async-start | bytes 4194304
  212.9 3.9 %copy-start.14 = (bf16[512,384]{0,1:T(8,128)(2,1)S(1)}, bf16[512,384]{0,1:T(8,128)(2,1)}, u32[]{:S(2)}) copy-start(bf16[512,384]{0,1:T(8,128)(2,1)} %copy-done.13) | copy-start | bytes 1179652
  213.6 10.4 %copy-start.15 = (bf16[6,64,512]{2,1,0:T(8,128)(2,1)}, bf16[6,64,512]{2,1,0:T(8,128)(2,1)S(1)}, u32[]{:S(2)}) copy-start(bf16[6,64,512]{2,1,0:T(8,128)(2,1)S(1)} %convolution_convert_fusion.12) | copy-start | bytes 1179652
  215.2 8.8 %collective-permute-start.10 = (bf16[256,768]{1,0:T(8,128)(2,1)S(1)}, bf16[256,768]{1,0:T(8,128)(2,1)S(1)}, u32[]{:S(2)}, u32[]{:S(2)}) collective-permute-start(bf16[256,768]{1,0:T(8,128)(2,1)S(1)} %convolution_convert_fusion.16), channel_id=1, source_target_pairs={{0,1},{1,0},{2,3},{3,2},{4,5},{5,4},{6,7},{7,6},{8,9},{9,8},{10,11... | collective-permute-start | bytes 1179656 | tf_op jit(solution)/shard_map/ppermute | solution.py:26
  227.0 9.8 %slice-start.2 = ((s8[6291456]{0:T(1024)(128)(4,1)}), s8[4194304]{0:T(1024)(128)(4,1)S(1)}, s32[]{:S(2)}) async-start(s8[6291456]{0:T(1024)(128)(4,1)} %bitcast.118), calls=%async_computation.8 | async-start | bytes 8388608
  227.0 9.8 %slice-start.3 = ((s8[6291456]{0:T(1024)(128)(4,1)}), s8[2097152]{0:T(1024)(128)(4,1)S(1)}, s32[]{:S(2)}) async-start(s8[6291456]{0:T(1024)(128)(4,1)} %bitcast.118), calls=%async_computation.9 | async-start | bytes 4194304
  227.0 7.8 %collective-permute-start.11 = (bf16[256,768]{1,0:T(8,128)(2,1)S(1)}, bf16[256,768]{1,0:T(8,128)(2,1)S(1)}, u32[]{:S(2)}, u32[]{:S(2)}) collective-permute-start(bf16[256,768]{1,0:T(8,128)(2,1)S(1)} %get-tuple-element.170), channel_id=1, source_target_pairs={{0,1},{1,0},{2,3},{3,2},{4,5},{5,4},{6,7},{7,6},{8,9},{9,8},{10,11... | collective-permute-start | bytes 1179656 | tf_op jit(solution)/shard_map/ppermute | solution.py:26
  236.7 2.5 copy-start.10
  240.9 2.7 copy-start.4
  246.7 2.5 copy-start.29
  246.7 2.5 copy-start.41
  246.7 2.5 copy-start.43
  249.2 3.0 copy-start.21
  249.3 3.0 copy-start.31
  249.3 3.0 copy-start.33
  249.3 3.0 copy-start.46
  259.7 25.9 %collective-permute-start.6 = (bf16[256,768]{1,0:T(8,128)(2,1)}, bf16[256,768]{1,0:T(8,128)(2,1)}, u32[]{:S(2)}, u32[]{:S(2)}) collective-permute-start(bf16[256,768]{1,0:T(8,128)(2,1)} %convolution_convert_fusion.14), channel_id=1, source_target_pairs={{0,1},{1,0},{2,3},{3,2},{4,5},{5,4},{6,7},{7,6},{8,9},{9,8},{10,11... | collective-permute-start | bytes 1179656 | tf_op jit(solution)/shard_map/ppermute | solution.py:26
  266.9 11.3 %collective-permute-start.12 = (bf16[256,768]{1,0:T(8,128)(2,1)}, bf16[256,768]{1,0:T(8,128)(2,1)}, u32[]{:S(2)}, u32[]{:S(2)}) collective-permute-start(bf16[256,768]{1,0:T(8,128)(2,1)} %fusion.49), channel_id=1, source_target_pairs={{0,1},{1,0},{2,3},{3,2},{4,5},{5,4},{6,7},{7,6},{8,9},{9,8},{10,11... | collective-permute-start | bytes 1179656 | tf_op jit(solution)/shard_map/ppermute | solution.py:26
  271.3 6.9 %copy-start.18 = (bf16[512,1152]{0,1:T(8,128)(2,1)S(1)}, bf16[512,1152]{0,1:T(8,128)(2,1)}, u32[]{:S(2)}) copy-start(bf16[512,1152]{0,1:T(8,128)(2,1)} %copy-done.17) | copy-start | bytes 3538948
  278.2 4.3 %copy-start.22 = (bf16[6,64,512]{2,1,0:T(8,128)(2,1)S(1)}, bf16[6,64,512]{2,1,0:T(8,128)(2,1)}, u32[]{:S(2)}) copy-start(bf16[6,64,512]{2,1,0:T(8,128)(2,1)} %fusion.61) | copy-start | bytes 1179652
  278.2 4.3 %copy-start.47 = (bf16[6,64,512]{2,1,0:T(8,128)(2,1)S(1)}, bf16[6,64,512]{2,1,0:T(8,128)(2,1)}, u32[]{:S(2)}) copy-start(bf16[6,64,512]{2,1,0:T(8,128)(2,1)} %convolution_convert_fusion.10) | copy-start | bytes 1179652
  280.8 4.9 %copy-start.6 = (f32[256,768]{1,0:T(8,128)S(1)}, f32[256,768]{1,0:T(8,128)}, u32[]{:S(2)}) copy-start(f32[256,768]{1,0:T(8,128)} %copy-done.5) | copy-start | bytes 2359300
  280.8 4.9 %copy-start.50 = (bf16[512,1024]{1,0:T(8,128)(2,1)S(1)}, bf16[512,1024]{1,0:T(8,128)(2,1)}, u32[]{:S(2)}) copy-start(bf16[512,1024]{1,0:T(8,128)(2,1)} %copy-done.48) | copy-start | bytes 3145732
  280.9 4.7 %collective-permute-start.14 = (f32[15,768]{1,0:T(8,128)S(1)}, f32[15,768]{1,0:T(8,128)S(1)}, u32[]{:S(2)}, u32[]{:S(2)}) collective-permute-start(f32[15,768]{1,0:T(8,128)S(1)} %pad_maximum_fusion.28), channel_id=1, source_target_pairs={{0,1},{1,0},{2,3},{3,2},{4,5},{5,4},{6,7},{7,6},{8,9},{9,8},{10,11... | collective-permute-start | bytes 138248 | tf_op jit(solution)/shard_map/ppermute | solution.py:56
  284.4 7.8 %collective-permute-start.13 = (bf16[256,768]{1,0:T(8,128)(2,1)S(1)}, bf16[256,768]{1,0:T(8,128)(2,1)S(1)}, u32[]{:S(2)}, u32[]{:S(2)}) collective-permute-start(bf16[256,768]{1,0:T(8,128)(2,1)S(1)} %convolution_convert_fusion.9), channel_id=1, source_target_pairs={{0,1},{1,0},{2,3},{3,2},{4,5},{5,4},{6,7},{7,6},{8,9},{9,8},{10,11... | collective-permute-start | bytes 1179656 | tf_op jit(solution)/shard_map/ppermute | solution.py:26
  285.6 3.3 collective-permute-start.15
  288.8 13.0 %copy-start.9 = (f32[256,768]{1,0:T(8,128)S(1)}, f32[256,768]{1,0:T(8,128)}, u32[]{:S(2)}) copy-start(f32[256,768]{1,0:T(8,128)} %get-tuple-element.171) | copy-start | bytes 2359300
  288.9 6.1 %collective-permute-start.16 = (f32[15,768]{1,0:T(8,128)S(1)}, f32[15,768]{1,0:T(8,128)S(1)}, u32[]{:S(2)}, u32[]{:S(2)}) collective-permute-start(f32[15,768]{1,0:T(8,128)S(1)} %add.217), channel_id=1, source_target_pairs={{0,4},{2,6},{4,0},{6,2},{8,12},{10,14},{12,8},{14,10},{16,20},{18,... | collective-permute-start | bytes 138248 | tf_op jit(solution)/shard_map/ppermute | solution.py:56
  294.9 4.2 %collective-permute-start.17 = (f32[15,768]{1,0:T(8,128)S(1)}, f32[15,768]{1,0:T(8,128)S(1)}, u32[]{:S(2)}, u32[]{:S(2)}) collective-permute-start(f32[15,768]{1,0:T(8,128)S(1)} %add.218), channel_id=1, source_target_pairs={{0,8},{2,10},{4,12},{6,14},{8,0},{10,2},{12,4},{14,6},{16,24},{18,... | collective-permute-start | bytes 138248 | tf_op jit(solution)/shard_map/ppermute | solution.py:56
  299.1 5.3 %collective-permute-start.18 = (f32[15,768]{1,0:T(8,128)S(1)}, f32[15,768]{1,0:T(8,128)S(1)}, u32[]{:S(2)}, u32[]{:S(2)}) collective-permute-start(f32[15,768]{1,0:T(8,128)S(1)} %add.219), channel_id=1, source_target_pairs={{0,16},{2,18},{4,20},{6,22},{8,24},{10,26},{12,28},{14,30},{16,0},... | collective-permute-start | bytes 138248 | tf_op jit(solution)/shard_map/ppermute | solution.py:56
  306.6 47.6 %copy-start.1 = (f32[32,12]{0,1:T(8,128)S(1)}, f32[32,12]{0,1:T(8,128)}, u32[]{:S(2)}) copy-start(f32[32,12]{0,1:T(8,128)} %param.26) | copy-start | bytes 4612
  (21 other events, 35.1 us)
Sparse Core Ops, SparseCore 0:
  10.9 44.8 all-gather.2
  58.6 64.7 all-gather.4
  197.2 73.3 reduce-scatter.4
  274.3 74.7 reduce-scatter.2
